TPU v7x, 256 devices: a whole 4x4x8 slice. The times are simulated.
256 devices in a mesh: param: 32 (over z, y_lo, core), sensor: 8 (over y_hi, x).
Axes of the slice: x: 4, y: 4 (y_hi: 2, y_lo: 2; y = y_hi * 2 + y_lo), z: 8, core: 2. Of those that a mesh axis runs over, the one named last changes fastest.
Arguments:
- kernel_spec: float32 [2, 96, 8, 512, 421], P(None, 'param', None, 'sensor'), may hold values from -1 to 1, as said below
- observed: float32 [512, 420], P('sensor'), may hold values from -6 to 6
- initial: float32 [96, 8, 420], P('param'), may hold values from 0 to 1, as said below
Outputs:
- sources: float32 [96, 8, 420], P('param')
- residual: float32 [512, 420], P('sensor')
Inputs may be any that keep to these rules, and one draw needn't show every extreme that they name: `kernel_spec`: real and imaginary parts of the transformed Green's function of each source point and sensor. `initial`: nonnegative starting source histories.
All inputs are finite; a program needn't handle non-finite values.
Results may differ from a plain program's by a relative error of at most 0.0001.
Values sent between devices are 32-bit elements; how exact they have to be, the bound alone decides.
No kernel may reach another device: no remote copies, remote signals or barrier semaphores. Data moves between devices by JAX's collectives and lax.ppermute only.
A program may use at most 64 MiB of HBM per device.

v0:
```python
import math

import jax
import jax.numpy as jnp
from jax import lax
from jax.sharding import PartitionSpec as P

ITERS = 2


HIGH = lax.Precision.HIGHEST
LAMBDA_REG = 0.5
TINY_TERM = 1e-06


def with_halo(block, sides, width):
    for axis, dim in sides:
        count = lax.axis_size(axis)
        forward = [(i, i + 1) for i in range(count - 1)]
        backward = [(target, source) for source, target in forward]
        low = lax.ppermute(
            lax.slice_in_dim(block, block.shape[dim] - width, None, axis=dim), axis, forward
        )
        high = lax.ppermute(lax.slice_in_dim(block, 0, width, axis=dim), axis, backward)
        block = jnp.concatenate([low, block, high], axis=dim)
    return block


def tables(length, freqs):
    times = lax.broadcasted_iota(jnp.int32, (length, freqs), 0)
    indices = lax.broadcasted_iota(jnp.int32, (length, freqs), 1)
    phase = times * indices % (2 * length)
    angle = phase.astype(jnp.float32) * (math.pi / length)
    return (jnp.cos(angle), jnp.sin(angle))


def spectrum(series, cosine, sine):
    real_part = jnp.einsum("...t,tf->...f", series, cosine, precision=HIGH)
    imag_part = -jnp.einsum("...t,tf->...f", series, sine, precision=HIGH)
    return (real_part, imag_part)


def series_of(real_part, imag_part, cosine, sine):
    length, freqs = cosine.shape
    column = lax.broadcasted_iota(jnp.int32, (freqs,), 0)
    weight = jnp.where((column == 0) | (column == freqs - 1), 1.0, 2.0) / (2.0 * length)
    first = jnp.einsum("...f,tf->...t", real_part * weight, cosine, precision=HIGH)
    second = jnp.einsum("...f,tf->...t", imag_part * weight, sine, precision=HIGH)
    return first - second


def predict(field, real_kernel, imag_kernel, cosine, sine):
    real_src, imag_src = spectrum(field, cosine, sine)
    real_out = jnp.einsum("cdsf,cdf->sf", real_kernel, real_src, precision=HIGH) - jnp.einsum(
        "cdsf,cdf->sf", imag_kernel, imag_src, precision=HIGH
    )
    imag_out = jnp.einsum("cdsf,cdf->sf", real_kernel, imag_src, precision=HIGH) + jnp.einsum(
        "cdsf,cdf->sf", imag_kernel, real_src, precision=HIGH
    )
    real_out, imag_out = lax.psum((real_out, imag_out), "param")
    return series_of(real_out, imag_out, cosine, sine)


def back_project(misfit, real_kernel, imag_kernel, cosine, sine):
    real_res, imag_res = spectrum(misfit, cosine, sine)
    real_out = jnp.einsum("cdsf,sf->cdf", real_kernel, real_res, precision=HIGH) + jnp.einsum(
        "cdsf,sf->cdf", imag_kernel, imag_res, precision=HIGH
    )
    imag_out = jnp.einsum("cdsf,sf->cdf", real_kernel, imag_res, precision=HIGH) - jnp.einsum(
        "cdsf,sf->cdf", imag_kernel, real_res, precision=HIGH
    )
    real_out, imag_out = lax.psum((real_out, imag_out), "sensor")
    return series_of(real_out, imag_out, cosine, sine)


def smoothing(field):
    padded = with_halo(field, (("param", 0),), 1)
    along = padded[2:] + padded[:-2]
    down_dip = jnp.pad(field, ((0, 0), (1, 1), (0, 0)))
    return 4.0 * field - along - down_dip[:, 2:] - down_dip[:, :-2]


def body(kernel_spec, observed, initial):
    cosine, sine = tables(observed.shape[1], kernel_spec.shape[4])
    real_kernel = kernel_spec[0]
    imag_kernel = kernel_spec[1]
    sensor_count = lax.axis_size("sensor")
    param_count = lax.axis_size("param")
    sources = initial
    residual = observed
    for iteration in range(ITERS):
        residual = predict(sources, real_kernel, imag_kernel, cosine, sine) - observed
        gradient = back_project(
            residual, real_kernel, imag_kernel, cosine, sine
        ) + LAMBDA_REG * smoothing(sources)
        image = predict(gradient, real_kernel, imag_kernel, cosine, sine)
        grad_sq, image_sq = lax.psum(
            (jnp.sum(gradient * gradient) / sensor_count, jnp.sum(image * image) / param_count),
            ("param", "sensor"),
        )
        alpha = grad_sq / (image_sq + 8.0 * LAMBDA_REG * grad_sq + TINY_TERM)
        sources = jnp.maximum(sources - alpha * gradient, 0.0)
    return (sources, residual)


def solution(mesh):
    placed = (P(None, "param", None, "sensor", None), P("sensor", None), P("param", None, None))
    return jax.shard_map(
        body,
        mesh=mesh,
        in_specs=placed,
        out_specs=(P("param", None, None), P("sensor", None)),
        check_vma=False,
    )
```

profile of v0, /device:TPU:1, one launch (start us, length us, event | category | flops | bytes accessed | tf_op | source)
XLA Modules:
  0.0 1373.7 jit_solution(17246897917068206060)
XLA Ops:
  7.2 4.9 fusion.50
  12.1 5.0 convolution_negate_fusion.5
  23.1 224.2 %all-reduce.23.cloned.1.call-done = (f32[64,421]{0,1:T(8,128)}, f32[64,421]{0,1:T(8,128)}) async-done(((f32[64,421]{0,1:T(8,128)}, f32[64,421]{0,1:T(8,128)}), (f32[64,421]{0,1:T(8,128)}, f32[64,421]{0,1:T(8,128)})) %all-reduce.23.cloned.1.call-update) | async-done | bytes 215568 | tf_op jit(solution)/shard_map/psum | solution.py:60
  247.3 5.2 fusion.69
  252.5 5.2 fusion.28
  266.4 4.7 fusion.1
  276.9 76.7 %all-reduce.27.cloned.1.call-done = (f32[3,8,421]{2,1,0:T(8,128)}, f32[3,8,421]{2,1,0:T(8,128)}) async-done(((f32[3,8,421]{2,1,0:T(8,128)}, f32[3,8,421]{2,1,0:T(8,128)}), (f32[3,8,421]{2,1,0:T(8,128)}, f32[3,8,421]{2,1,0:T(8,128)})) %all-reduce.27.cloned.1.call-update) | async-done | bytes 80848 | tf_op jit(solution)/shard_map/psum | solution.py:72
  353.6 5.4 fusion.48
  359.0 5.7 multiply_reduce_fusion.1
  377.1 223.2 %all-reduce.21.cloned.1.call-done = (f32[64,421]{0,1:T(8,128)}, f32[64,421]{0,1:T(8,128)}) async-done(((f32[64,421]{0,1:T(8,128)}, f32[64,421]{0,1:T(8,128)}), (f32[64,421]{0,1:T(8,128)}, f32[64,421]{0,1:T(8,128)})) %all-reduce.21.cloned.1.call-update) | async-done | bytes 215568 | tf_op jit(solution)/shard_map/psum | solution.py:60
  600.3 5.2 fusion.62
  605.5 5.9 fusion.85
  612.0 77.1 %all-reduce.3 = (f32[]{:T(128)}, f32[]{:T(128)}) all-reduce(f32[]{:T(128)S(6)} %div.49, f32[]{:T(128)S(6)} %div.50), channel_id=1, replica_groups=mesh['param'=32,'sensor'=8] {'param','sensor'}, use_global_device_ids=true, to_apply=%region_5.6 | all-reduce | flops 2 | bytes 16 | tf_op jit(solution)/shard_map/psum | solution.py:97
  705.6 216.4 %all-reduce.19.cloned.1.call-done = (f32[64,421]{0,1:T(8,128)}, f32[64,421]{0,1:T(8,128)}) async-done(((f32[64,421]{0,1:T(8,128)}, f32[64,421]{0,1:T(8,128)}), (f32[64,421]{0,1:T(8,128)}, f32[64,421]{0,1:T(8,128)})) %all-reduce.19.cloned.1.call-update) | async-done | bytes 215568 | tf_op jit(solution)/shard_map/psum | solution.py:60
  922.0 5.2 fusion.64
  927.2 5.2 fusion.29
  941.2 4.7 fusion.3
  951.6 76.8 %all-reduce.25.cloned.1.call-done = (f32[3,8,421]{2,1,0:T(8,128)}, f32[3,8,421]{2,1,0:T(8,128)}) async-done(((f32[3,8,421]{2,1,0:T(8,128)}, f32[3,8,421]{2,1,0:T(8,128)}), (f32[3,8,421]{2,1,0:T(8,128)}, f32[3,8,421]{2,1,0:T(8,128)})) %all-reduce.25.cloned.1.call-update) | async-done | bytes 80848 | tf_op jit(solution)/shard_map/psum | solution.py:72
  1028.3 5.5 fusion.44
  1033.8 5.7 multiply_reduce_fusion
  1051.9 223.5 %all-reduce.17.cloned.1.call-done = (f32[64,421]{0,1:T(8,128)}, f32[64,421]{0,1:T(8,128)}) async-done(((f32[64,421]{0,1:T(8,128)}, f32[64,421]{0,1:T(8,128)}), (f32[64,421]{0,1:T(8,128)}, f32[64,421]{0,1:T(8,128)})) %all-reduce.17.cloned.1.call-update) | async-done | bytes 215568 | tf_op jit(solution)/shard_map/psum | solution.py:60
  1275.4 5.2 fusion.66
  1280.6 5.9 fusion.88
  1287.1 76.6 %all-reduce.2 = (f32[]{:T(128)}, f32[]{:T(128)}) all-reduce(f32[]{:T(128)S(6)} %div.52, f32[]{:T(128)S(6)} %div.53), channel_id=1, replica_groups=mesh['param'=32,'sensor'=8] {'param','sensor'}, use_global_device_ids=true, to_apply=%region_15.16 | all-reduce | flops 2 | bytes 16 | tf_op jit(solution)/shard_map/psum | solution.py:97
  (82 shorter events, 72.8 us)
Async XLA Ops:
  7.2 240.2 %all-reduce.23.cloned.1.call-start = ((), (), s32[]{:S(2)}) async-start(), calls=%async_computation.3 | async-start | bytes 868352 | tf_op jit(solution)/shard_map/psum | solution.py:60
  21.1 231.4 %copy-start.1 = (f32[64,420]{1,0:T(8,128)S(1)}, f32[64,420]{1,0:T(8,128)}, u32[]{:S(2)}) copy-start(f32[64,420]{1,0:T(8,128)} %param.4) | copy-start | bytes 322564
  22.5 331.0 %all-reduce.27.cloned.1.call-start = ((), (), s32[]{:S(2)}) async-start(), calls=%async_computation.5 | async-start | bytes 196608 | tf_op jit(solution)/shard_map/psum | solution.py:72
  266.4 6.1 copy-start
  266.4 106.6 %slice-start = ((s8[6291456]{0:T(1024)(128)(4,1)}), s8[2097152]{0:T(1024)(128)(4,1)S(1)}, s32[]{:S(2)}) async-start(s8[6291456]{0:T(1024)(128)(4,1)} %bitcast.228), calls=%async_computation.6 | async-start | bytes 4194304
  272.4 327.9 %all-reduce.21.cloned.1.call-start = ((), (), s32[]{:S(2)}) async-start(), calls=%async_computation.2 | async-start | bytes 868352 | tf_op jit(solution)/shard_map/psum | solution.py:60
  272.5 86.5 %collective-permute-start.1 = (f32[1,8,420]{2,1,0:T(8,128)S(1)}, f32[1,8,420]{2,1,0:T(8,128)S(1)}, u32[]{:S(2)}, u32[]{:S(2)}) collective-permute-start(f32[1,8,420]{2,1,0:T(8,128)S(1)} %get-tuple-element.57), channel_id=1, source_target_pairs={{0,8},{8,16},{16,24},{24,32},{32,40},{40,48},{48,56},{56,64},{64,7... | collective-permute-start | bytes 40328 | tf_op jit(solution)/shard_map/ppermute | solution.py:21
  274.9 84.2 %collective-permute-start = (f32[1,8,420]{2,1,0:T(8,128)S(1)}, f32[1,8,420]{2,1,0:T(8,128)S(1)}, u32[]{:S(2)}, u32[]{:S(2)}) collective-permute-start(f32[1,8,420]{2,1,0:T(8,128)S(1)} %get-tuple-element.56), channel_id=1, source_target_pairs={{8,0},{16,8},{24,16},{32,24},{40,32},{48,40},{56,48},{64,56},{72,6... | collective-permute-start | bytes 40328 | tf_op jit(solution)/shard_map/ppermute | solution.py:24
  353.6 19.4 %slice-start.1 = ((s8[6291456]{0:T(1024)(128)(4,1)}), s8[4194304]{0:T(1024)(128)(4,1)S(1)}, s32[]{:S(2)}) async-start(s8[6291456]{0:T(1024)(128)(4,1)} %bitcast.228), calls=%async_computation.7 | async-start | bytes 8388608
  376.2 545.9 %all-reduce.19.cloned.1.call-start = ((), (), s32[]{:S(2)}) async-start(), calls=%async_computation.1 | async-start | bytes 868352 | tf_op jit(solution)/shard_map/psum | solution.py:60
  705.4 323.0 %all-reduce.25.cloned.1.call-start = ((), (), s32[]{:S(2)}) async-start(), calls=%async_computation.4 | async-start | bytes 196608 | tf_op jit(solution)/shard_map/psum | solution.py:72
  932.5 13.4 copy-start.2
  941.2 106.9 %slice-start.2 = ((s8[6291456]{0:T(1024)(128)(4,1)}), s8[2097152]{0:T(1024)(128)(4,1)S(1)}, s32[]{:S(2)}) async-start(s8[6291456]{0:T(1024)(128)(4,1)} %bitcast.230), calls=%async_computation.8 | async-start | bytes 4194304
  947.2 328.2 %all-reduce.17.cloned.1.call-start = ((), (), s32[]{:S(2)}) async-start(), calls=%async_computation | async-start | bytes 868352 | tf_op jit(solution)/shard_map/psum | solution.py:60
  947.3 86.6 %collective-permute-start.3 = (f32[1,8,420]{2,1,0:T(8,128)S(1)}, f32[1,8,420]{2,1,0:T(8,128)S(1)}, u32[]{:S(2)}, u32[]{:S(2)}) collective-permute-start(f32[1,8,420]{2,1,0:T(8,128)S(1)} %get-tuple-element.55), channel_id=1, source_target_pairs={{0,8},{8,16},{16,24},{24,32},{32,40},{40,48},{48,56},{56,64},{64,7... | collective-permute-start | bytes 40328 | tf_op jit(solution)/shard_map/ppermute | solution.py:21
  949.6 84.2 %collective-permute-start.2 = (f32[1,8,420]{2,1,0:T(8,128)S(1)}, f32[1,8,420]{2,1,0:T(8,128)S(1)}, u32[]{:S(2)}, u32[]{:S(2)}) collective-permute-start(f32[1,8,420]{2,1,0:T(8,128)S(1)} %get-tuple-element.54), channel_id=1, source_target_pairs={{8,0},{16,8},{24,16},{32,24},{40,32},{48,40},{56,48},{64,56},{72,6... | collective-permute-start | bytes 40328 | tf_op jit(solution)/shard_map/ppermute | solution.py:24
  1028.3 19.8 %slice-start.3 = ((s8[6291456]{0:T(1024)(128)(4,1)}), s8[4194304]{0:T(1024)(128)(4,1)S(1)}, s32[]{:S(2)}) async-start(s8[6291456]{0:T(1024)(128)(4,1)} %bitcast.230), calls=%async_computation.9 | async-start | bytes 8388608
Sparse Core Ops, SparseCore 0:
  22.7 224.6 all-reduce.22
  272.6 80.9 all-reduce.26
  376.3 223.9 all-reduce.20
  705.5 216.4 all-reduce.18
  947.3 80.9 all-reduce.24
  1051.4 223.9 all-reduce.16
where the time goes:
time: 1380 us; the launch traced here: 1370 us
  waiting for transfers between devices  1040 us (75%)
  blocking collectives  154 us (11%)
  matrix products  118 us (9%)
  other arithmetic  28 us (2%)
  between operations  21.7 us (2%)
    psum x4, waiting for transfers between devices, predict(): real_out, imag_out = lax.psum((real_out, imag_out), 'param')  887 us
    psum x2, blocking collectives, body(): lax.psum((jnp.sum(gradient * gradient) / sensor_count, jnp.sum(image * im...  154 us
    psum x2, waiting for transfers between devices, back_project(): real_out, imag_out = lax.psum((real_out, imag_out), 'sensor')  153 us
    dot_general x6, matrix products, series_of(): jnp.einsum('...f,tf->...t', imag_part * weight, sine, precision=HIGH)  33.7 us
    dot_general x6, matrix products, series_of(): jnp.einsum('...f,tf->...t', real_part * weight, cosine, precision=HIGH)  31.7 us
  transfers between devices with their start and end apart: 10, of which 6 were waited for; matrix products, arithmetic and copies ran while one was open for 1% of the time, Pallas kernels for 0%

commit v1 on v0

v1 whole, which is shorter than its diff:
```python
import functools
import math

import jax
import jax.numpy as jnp
import numpy as np
from jax import lax
from jax.experimental import pallas as pl
from jax.experimental.pallas import tpu as pltpu
from jax.sharding import PartitionSpec as P

ITERS = 2
LAMBDA_REG = 0.5
TINY_TERM = 1e-06
LANES = 128
ROWS = 8
F32 = jnp.float32
BF16 = jnp.bfloat16
VMEM_LIMIT = 20 * 1024 * 1024


def dft_table(steps, freqs, pad):
    index = np.arange(pad, dtype=np.int64)
    phase = (index[:, None] * index[None, :]) % (2 * steps)
    angle = phase * (math.pi / steps)
    inside = (index[:, None] < freqs) & (index[None, :] < freqs)
    whole = np.concatenate(
        [np.where(inside, np.cos(angle), 0.0), np.where(inside, -np.sin(angle), 0.0)], axis=1
    )
    high = whole.astype(np.float32).astype(BF16)
    low = (whole - high.astype(np.float64)).astype(np.float32).astype(BF16)
    return high, low


def split(x):
    high = x.astype(BF16)
    low = (x - high.astype(F32)).astype(BF16)
    return high, low


def product(x, high_ref, low_ref, columns):
    xh, xl = split(x)
    high = high_ref[:, columns]
    dot = functools.partial(jnp.dot, preferred_element_type=F32)
    return dot(xh, high) + dot(xl, high) + dot(xh, low_ref[:, columns])


def to_series(real_part, imag_part, high_ref, low_ref, steps):
    pad = real_part.shape[1]
    column = lax.broadcasted_iota(jnp.int32, (1, pad), 1)
    weight = jnp.where((column == 0) | (column == steps), 1.0, 2.0) / (2.0 * steps)
    out = product(real_part * weight, high_ref, low_ref, slice(0, pad))
    out += product(imag_part * weight, high_ref, low_ref, slice(pad, 2 * pad))
    return jnp.where(column < steps, out, 0.0)


def lane_blocks(freqs):
    return [(start, min(LANES, freqs - start)) for start in range(0, freqs, LANES)]


def forward_map(field, k_ref, high_ref, low_ref, xs_ref, ys_ref, out_ref, steps):
    _, cols, dips, sensors, freqs = k_ref.shape
    pad = field.shape[1]
    xs_ref[...] = product(field, high_ref, low_ref, slice(0, 2 * pad)).reshape(cols, dips, 2 * pad)
    tail = lane_blocks(freqs)[-1][0]
    ys_ref[:, tail:pad] = jnp.zeros((sensors, pad - tail), F32)
    ys_ref[:, pad + tail :] = jnp.zeros((sensors, pad - tail), F32)
    height = min(32, sensors)
    for start, width in lane_blocks(freqs):
        for top in range(0, sensors, height):

            def column(c, acc):
                real, imag = acc
                for d in range(dips):
                    kr = k_ref[0, c, d, top : top + height, start : start + width]
                    ki = k_ref[1, c, d, top : top + height, start : start + width]
                    xr = xs_ref[c, d : d + 1, start : start + width]
                    xi = xs_ref[c, d : d + 1, pad + start : pad + start + width]
                    real = real + kr * xr - ki * xi
                    imag = imag + kr * xi + ki * xr
                return real, imag

            zero = jnp.zeros((height, width), F32)
            real, imag = lax.fori_loop(0, cols, column, (zero, zero))
            ys_ref[top : top + height, start : start + width] = real
            ys_ref[top : top + height, pad + start : pad + start + width] = imag
    series = to_series(ys_ref[:, :pad], ys_ref[:, pad:], high_ref, low_ref, steps)
    tiles = pad // LANES
    for o in range(sensors // ROWS):
        for t in range(tiles):
            out_ref[o * tiles + t] = series[o * ROWS : (o + 1) * ROWS, t * LANES : (t + 1) * LANES]


def first_kernel(steps, s_ref, k_ref, high_ref, low_ref, out_ref, xs_ref, ys_ref):
    forward_map(s_ref[...], k_ref, high_ref, low_ref, xs_ref, ys_ref, out_ref, steps)


def stepped(s_ref, g_ref, sums_ref):
    sums = jnp.sum(sums_ref[...], axis=0)
    image_sq = sums[:, :1]
    grad_sq = sums[:, LANES // 2 : LANES // 2 + 1]
    alpha = grad_sq / (image_sq + 8.0 * LAMBDA_REG * grad_sq + TINY_TERM)
    return jnp.maximum(s_ref[...] - alpha * g_ref[...], 0.0)


def step_kernel(steps, s_ref, g_ref, sums_ref, k_ref, high_ref, low_ref, out_ref, new_ref, xs_ref, ys_ref):
    new = stepped(s_ref, g_ref, sums_ref)
    new_ref[...] = new
    forward_map(new, k_ref, high_ref, low_ref, xs_ref, ys_ref, out_ref, steps)


def last_kernel(s_ref, g_ref, sums_ref, out_ref):
    new = stepped(s_ref, g_ref, sums_ref)
    cols, dips, steps = out_ref.shape
    for c in range(cols):
        out_ref[c] = new[c * dips : (c + 1) * dips, :steps]


def misfit_kernel(parts_ref, observed_ref, out_ref):
    misfit = jnp.sum(parts_ref[...], axis=0) - observed_ref[...]
    out_ref[...] = jnp.broadcast_to(misfit[None], out_ref.shape)


def adjoint_kernel(steps, r_ref, k_ref, high_ref, low_ref, out_ref, res_ref, ys_ref, xs_ref):
    _, cols, dips, sensors, freqs = k_ref.shape
    pad = xs_ref.shape[2] // 2
    tiles = pad // LANES
    for o in range(sensors // ROWS):
        for t in range(tiles):
            width = min(LANES, steps - t * LANES)
            res_ref[o * ROWS : (o + 1) * ROWS, t * LANES : t * LANES + width] = r_ref[o * tiles + t][:, :width]
    rows = [
        jnp.concatenate([r_ref[o * tiles + t] for t in range(tiles)], axis=1)
        for o in range(sensors // ROWS)
    ]
    misfit = jnp.concatenate(rows, axis=0)
    ys_ref[...] = product(misfit, high_ref, low_ref, slice(0, 2 * pad))
    tail = lane_blocks(freqs)[-1][0]
    xs_ref[:, :, tail:pad] = jnp.zeros((cols, dips, pad - tail), F32)
    xs_ref[:, :, pad + tail :] = jnp.zeros((cols, dips, pad - tail), F32)
    for start, width in lane_blocks(freqs):
        rr = [ys_ref[top : top + ROWS, start : start + width] for top in range(0, sensors, ROWS)]
        ri = [ys_ref[top : top + ROWS, pad + start : pad + start + width] for top in range(0, sensors, ROWS)]

        def column(c, carry):
            for d in range(dips):
                real = jnp.zeros((ROWS, width), F32)
                imag = jnp.zeros((ROWS, width), F32)
                for i in range(sensors // ROWS):
                    kr = k_ref[0, c, d, i * ROWS : (i + 1) * ROWS, start : start + width]
                    ki = k_ref[1, c, d, i * ROWS : (i + 1) * ROWS, start : start + width]
                    real = real + kr * rr[i] + ki * ri[i]
                    imag = imag + kr * ri[i] - ki * rr[i]
                xs_ref[c, d : d + 1, start : start + width] = jnp.sum(real, axis=0, keepdims=True)
                xs_ref[c, d : d + 1, pad + start : pad + start + width] = jnp.sum(imag, axis=0, keepdims=True)
            return carry

        lax.fori_loop(0, cols, column, 0)
    spectra = xs_ref[...].reshape(cols * dips, 2 * pad)
    series = to_series(spectra[:, :pad], spectra[:, pad:], high_ref, low_ref, steps)
    for i in range(out_ref.shape[0]):
        out_ref[i] = series


def gradient_kernel(
    steps, parts_ref, s_ref, below_ref, above_ref, k_ref, high_ref, low_ref, out_ref, g_ref, xs_ref, ys_ref
):
    cols, dips = k_ref.shape[1:3]
    field = s_ref[...]
    count = cols * dips
    earlier = jnp.concatenate([below_ref[...], field[: count - dips]], axis=0)
    later = jnp.concatenate([field[dips:], above_ref[...]], axis=0)
    dip = lax.broadcasted_iota(jnp.int32, field.shape, 0) % dips
    upper = jnp.where(dip == 0, 0.0, pltpu.roll(field, 1, 0))
    lower = jnp.where(dip == dips - 1, 0.0, pltpu.roll(field, count - 1, 0))
    smooth = 4.0 * field - (earlier + later) - lower - upper
    gradient = jnp.sum(parts_ref[...], axis=0) + LAMBDA_REG * smooth
    g_ref[...] = gradient
    forward_map(gradient, k_ref, high_ref, low_ref, xs_ref, ys_ref, out_ref, steps)


def squares_kernel(copies, parts_ref, g_ref, out_ref):
    image = jnp.sum(parts_ref[...], axis=0)
    gradient = g_ref[...]
    image_sq = jnp.sum(image * image, keepdims=True)
    grad_sq = jnp.sum(gradient * gradient, keepdims=True) * (1.0 / copies)
    lane = lax.broadcasted_iota(jnp.int32, (1, LANES), 1)
    both = jnp.where(lane < LANES // 2, image_sq, grad_sq)
    out_ref[...] = jnp.broadcast_to(both[None], out_ref.shape)


def shape(*dims):
    return jax.ShapeDtypeStruct(dims, F32)


def call(kernel, out_shape, scratch=()):
    return pl.pallas_call(
        kernel,
        out_shape=out_shape,
        scratch_shapes=[pltpu.VMEM(dims, F32) for dims in scratch],
        compiler_params=pltpu.CompilerParams(vmem_limit_bytes=VMEM_LIMIT),
    )


def body(kernel_spec, observed, initial):
    _, cols, dips, sensors, freqs = kernel_spec.shape
    steps = observed.shape[1]
    points = cols * dips
    pad = -(-freqs // LANES) * LANES
    tiles = pad // LANES
    params = lax.axis_size("param")
    groups = lax.axis_size("sensor")
    assert params == sensors // ROWS * tiles and dips == ROWS
    high, low = (jnp.asarray(part) for part in dft_table(steps, freqs, pad))
    me = lax.axis_index("param")
    own = lax.dynamic_slice(
        jnp.pad(observed, ((0, 0), (0, pad - steps))),
        (me // tiles * ROWS, me % tiles * LANES),
        (ROWS, LANES),
    )
    tiled = shape(params, ROWS, LANES)
    both = [(cols, dips, 2 * pad), (sensors, 2 * pad)]
    swap = functools.partial(lax.all_to_all, split_axis=0, concat_axis=0)
    up = [(i, i + 1) for i in range(params - 1)]
    down = [(i + 1, i) for i in range(params - 1)]

    sources = jnp.pad(initial.reshape(points, steps), ((0, 0), (0, pad - steps)))
    for iteration in range(ITERS):
        if iteration == 0:
            parts = call(functools.partial(first_kernel, steps), tiled, both)(sources, kernel_spec, high, low)
        else:
            parts, sources = call(
                functools.partial(step_kernel, steps), (tiled, shape(points, pad)), both
            )(sources, gradient, sums, kernel_spec, high, low)
        below = lax.ppermute(sources[points - dips :], "param", up)
        above = lax.ppermute(sources[:dips], "param", down)
        misfit = call(misfit_kernel, tiled)(swap(parts, "param"), own)
        partial, residual = call(
            functools.partial(adjoint_kernel, steps),
            (shape(groups, points, pad), shape(sensors, steps)),
            both[::-1],
        )(swap(misfit, "param"), kernel_spec, high, low)
        image, gradient = call(
            functools.partial(gradient_kernel, steps), (tiled, shape(points, pad)), both
        )(swap(partial, "sensor"), sources, below, above, kernel_spec, high, low)
        squares = call(functools.partial(squares_kernel, groups), shape(params * groups, 1, LANES))(
            swap(image, "param"), gradient
        )
        sums = swap(squares, ("param", "sensor"))
    sources = call(last_kernel, shape(cols, dips, steps))(sources, gradient, sums)
    return (sources, residual)


def solution(mesh):
    placed = (P(None, "param", None, "sensor", None), P("sensor", None), P("param", None, None))
    return jax.shard_map(
        body,
        mesh=mesh,
        in_specs=placed,
        out_specs=(P("param", None, None), P("sensor", None)),
        check_vma=False,
    )
```

time: 1380 us -> 192 us (0.14)
  waiting for transfers between devices: 1040 us -> 19.1 us
  matrix products: 118 us -> 0 us
  blocking collectives: 154 us -> 106 us
  other arithmetic: 28 us -> 0 us
  starting transfers between devices: 9.84 us -> 31.7 us
  between operations: 21.7 us -> 0.82 us
  Pallas kernels: 0 us -> 18.9 us
    psum x6 -> x0, waiting for transfers between devices: 1040 us -> none  [the longest x4 887 us: predict(): real_out, imag_out = lax.psum((real_out, imag_out), 'param')]
    psum x2 -> x0, blocking collectives: 154 us -> none  [body(): lax.psum((jnp.sum(gradient * gradient) / sensor_count, jnp.sum(image * im...]
    dot_general x24 -> x0, matrix products: 118 us -> none  [the longest x6 33.7 us: series_of(): jnp.einsum('...f,tf->...t', imag_part * weight, sine, precision=HIGH)]
    all_to_all x0 -> x7, blocking collectives: none -> 106 us  [the longest x2 42.7 us: body(): sums = swap(squares, ('param', 'sensor'))]
    all_to_all x0 -> x3, starting transfers between devices: none -> 21.1 us  [the longest x1 11.3 us: body(): misfit = call(misfit_kernel, tiled)(swap(parts, 'param'), own)]
    pallas_call x0 -> x11, Pallas kernels: none -> 18.9 us  [the longest x2 6.72 us: body(): call(functools.partial(adjoint_kernel, steps), (shape(groups, points, pad...]
  transfers between devices with their start and end apart: 10 -> 7, of which waited for: 6 -> 5; matrix products, arithmetic and copies ran while one was open for 1% -> 0% of each run, Pallas kernels for 0% -> 0%
where the time goes in v1:
time: 192 us; the launch traced here: 191 us
  blocking collectives  106 us (55%)
  starting transfers between devices  31.7 us (17%)
  waiting for transfers between devices  19.1 us (10%)
  Pallas kernels  18.9 us (10%)
  local copies, waits for them, and re-layouts  14.4 us (8%)
    all_to_all x2, blocking collectives, body(): sums = swap(squares, ('param', 'sensor'))  42.7 us
    all_to_all x2, blocking collectives, body(): swap(image, 'param')  25.7 us
    all_to_all x2, blocking collectives, body(): swap(misfit, 'param')  25 us
    unnamed x22, local copies, waits for them, and re-layouts  13.6 us
    all_to_all x1, blocking collectives, body(): misfit = call(misfit_kernel, tiled)(swap(parts, 'param'), own)  13 us
    all_to_all x1, starting transfers between devices, body(): misfit = call(misfit_kernel, tiled)(swap(parts, 'param'), own)  11.3 us
    all_to_all x2, starting transfers between devices, body(): swap(partial, 'sensor')  9.81 us
    all_to_all x1, waiting for transfers between devices, body(): misfit = call(misfit_kernel, tiled)(swap(parts, 'param'), own)  9.17 us
  transfers between devices with their start and end apart: 7, of which 5 were waited for; matrix products, arithmetic and copies ran while one was open for 0% of the time, Pallas kernels for 0%

profile of v1, /device:TPU:1, one launch (start us, length us, event | category | flops | bytes accessed | tf_op | source)
XLA Modules:
  0.0 191.4 jit_solution(982435021315940016)
XLA Ops:
  1.4 2.8 %copy-done = f32[2,3,8,64,421]{4,3,2,1,0:T(8,128)S(1)} copy-done((f32[2,3,8,64,421]{4,3,2,1,0:T(8,128)S(1)}, f32[2,3,8,64,421]{4,3,2,1,0:T(8,128)}, u32[]{:S(2)}) %copy-start) | copy-done | bytes 5173272
  6.7 3.0 %shard_map.68 = f32[32,8,128]{2,1,0:T(8,128)} custom-call(f32[24,512]{1,0:T(8,128)S(1)} %pad.8.s_ref, f32[2,3,8,64,421]{4,3,2,1,0:T(8,128)S(1)} %copy-done, bf16[512,1024]{1,0:T(8,128)(2,1)S(1)} %copy-done.5, bf16[512,1024]{1,0:T(8,128)(2,1)S(1)} %copy-done.7), custom_call_target="tpu_custom_call" | custom-call | tf_op jit(solution)/shard_map/pallas_call | solution.py:230
  9.7 11.3 %all-to-all-start = ((f32[32,8,128]{2,1,0:T(8,128)}), f32[32,8,128]{2,1,0:T(8,128)S(1)}, u32[]{:S(2)}, u32[]{:S(2)}) async-start(f32[32,8,128]{2,1,0:T(8,128)} %shard_map.68), calls=%async_computation | async-start | bytes 262144 | tf_op jit(solution)/shard_map/all_to_all | solution.py:237
  21.0 9.2 %all-to-all-done.parts_ref = f32[32,8,128]{2,1,0:T(8,128)S(1)} async-done(((f32[32,8,128]{2,1,0:T(8,128)}), f32[32,8,128]{2,1,0:T(8,128)S(1)}, u32[]{:S(2)}, u32[]{:S(2)}) %all-to-all-start) | async-done | bytes 131104 | tf_op jit(solution)/shard_map/all_to_all | solution.py:237
  30.2 12.5 %all_to_all.50.r_ref = f32[32,8,128]{2,1,0:T(8,128)S(1)} all-to-all(f32[32,8,128]{2,1,0:T(8,128)S(1)} %shard_map.69), channel_id=1, replica_groups=mesh['param'=32,'sensor'=8] {'param'}, dimensions={0} | all-to-all | bytes 262144 | tf_op jit(solution)/shard_map/all_to_all | solution.py:242
  42.8 2.8 %copy-done.1 = f32[2,3,8,64,421]{4,3,2,1,0:T(8,128)S(1)} copy-done((f32[2,3,8,64,421]{4,3,2,1,0:T(8,128)S(1)}, f32[2,3,8,64,421]{4,3,2,1,0:T(8,128)}, u32[]{:S(2)}) %copy-start.1) | copy-done | bytes 5173272
  45.6 3.4 %shard_map.70 = (f32[8,24,512]{2,1,0:T(8,128)}, f32[64,420]{1,0:T(8,128)}) custom-call(f32[32,8,128]{2,1,0:T(8,128)S(1)} %all_to_all.50.r_ref, f32[2,3,8,64,421]{4,3,2,1,0:T(8,128)S(1)} %copy-done.1, bf16[512,1024]{1,0:T(8,128)(2,1)S(1)} %copy-done.6, bf16[512,1024]{1,0:T(8,128)(2,1)S(1)} %copy-done.8), custom_call_target="tpu_custom_call" | custom-call | tf_op jit(solution)/shard_map/pallas_call | solution.py:238
  48.9 6.4 %all-to-all-start.2 = ((f32[8,24,512]{2,1,0:T(8,128)}), f32[8,24,512]{2,1,0:T(8,128)S(1)}, u32[]{:S(2)}, u32[]{:S(2)}) async-start(f32[8,24,512]{2,1,0:T(8,128)} %get-tuple-element.11), calls=%async_computation.2 | async-start | bytes 786432 | tf_op jit(solution)/shard_map/all_to_all | solution.py:245
  55.3 3.2 %collective-permute-start = (f32[8,512]{1,0:T(8,128)S(1)}, f32[8,512]{1,0:T(8,128)S(1)}, u32[]{:S(2)}, u32[]{:S(2)}) collective-permute-start(f32[8,512]{1,0:T(8,128)S(1)} %get-tuple-element.23), channel_id=1, source_target_pairs={{0,8},{8,16},{16,24},{24,32},{32,40},{40,48},{48,56},{56,64},{64,7... | collective-permute-start | bytes 49160 | tf_op jit(solution)/shard_map/ppermute | solution.py:235
  60.5 3.4 %collective-permute-done.1.above_ref = f32[8,512]{1,0:T(8,128)S(1)} collective-permute-done((f32[8,512]{1,0:T(8,128)S(1)}, f32[8,512]{1,0:T(8,128)S(1)}, u32[]{:S(2)}, u32[]{:S(2)}) %collective-permute-start.1) | collective-permute-done | bytes 16416 | tf_op jit(solution)/shard_map/ppermute | solution.py:236
  65.6 2.8 %copy-done.2 = f32[2,3,8,64,421]{4,3,2,1,0:T(8,128)S(1)} copy-done((f32[2,3,8,64,421]{4,3,2,1,0:T(8,128)S(1)}, f32[2,3,8,64,421]{4,3,2,1,0:T(8,128)}, u32[]{:S(2)}) %copy-start.2) | copy-done | bytes 5173272
  70.8 12.8 %all_to_all.51.parts_ref = f32[32,8,128]{2,1,0:T(8,128)S(1)} all-to-all(f32[32,8,128]{2,1,0:T(8,128)S(1)} %get-tuple-element.13), channel_id=1, replica_groups=mesh['param'=32,'sensor'=8] {'param'}, dimensions={0} | all-to-all | bytes 262144 | tf_op jit(solution)/shard_map/all_to_all | solution.py:247
  83.8 21.4 %all_to_all.52.sums_ref = f32[256,1,128]{2,1,0:T(1,128)S(1)} all-to-all(f32[256,1,128]{2,1,0:T(1,128)S(1)} %shard_map.72), channel_id=1, replica_groups=mesh['param'=32,'sensor'=8] {'param','sensor'}, dimensions={0} | all-to-all | bytes 262144 | tf_op jit(solution)/shard_map/all_to_all | solution.py:249
  105.3 2.9 %shard_map.73 = (f32[32,8,128]{2,1,0:T(8,128)S(1)}, f32[24,512]{1,0:T(8,128)S(1)}) custom-call(f32[24,512]{1,0:T(8,128)S(1)} %pad.8.s_ref, f32[24,512]{1,0:T(8,128)S(1)} %get-tuple-element.12.g_ref, f32[256,1,128]{2,1,0:T(1,128)S(1)} %all_to_all.52.sums_ref, f32[2,3,8,64,421]{4,3,2,1,0:T(8,128)S(1)} %copy-done.3, bf16[512,1024]{1,0:T(8,128)(2,1)S(1)} %copy-done.6, ...), custom_call_target="tpu_custom_call" | custom-call | tf_op jit(solution)/shard_map/pallas_call | solution.py:232
  108.2 13.0 %all_to_all.53.parts_ref = f32[32,8,128]{2,1,0:T(8,128)S(1)} all-to-all(f32[32,8,128]{2,1,0:T(8,128)S(1)} %get-tuple-element.15), channel_id=1, replica_groups=mesh['param'=32,'sensor'=8] {'param'}, dimensions={0} | all-to-all | bytes 262144 | tf_op jit(solution)/shard_map/all_to_all | solution.py:237
  121.2 12.4 %all_to_all.54.r_ref = f32[32,8,128]{2,1,0:T(8,128)S(1)} all-to-all(f32[32,8,128]{2,1,0:T(8,128)S(1)} %shard_map.74), channel_id=1, replica_groups=mesh['param'=32,'sensor'=8] {'param'}, dimensions={0} | all-to-all | bytes 262144 | tf_op jit(solution)/shard_map/all_to_all | solution.py:242
  133.7 3.4 %shard_map.75 = (f32[8,24,512]{2,1,0:T(8,128)}, f32[64,420]{1,0:T(8,128)}) custom-call(f32[32,8,128]{2,1,0:T(8,128)S(1)} %all_to_all.54.r_ref, f32[2,3,8,64,421]{4,3,2,1,0:T(8,128)S(1)} %copy-done.3, bf16[512,1024]{1,0:T(8,128)(2,1)S(1)} %copy-done.6, bf16[512,1024]{1,0:T(8,128)(2,1)S(1)} %copy-done.8), custom_call_target="tpu_custom_call" | custom-call | tf_op jit(solution)/shard_map/pallas_call | solution.py:238
  137.0 3.5 %all-to-all-start.7 = ((f32[8,24,512]{2,1,0:T(8,128)}), f32[8,24,512]{2,1,0:T(8,128)S(1)}, u32[]{:S(2)}, u32[]{:S(2)}) async-start(f32[8,24,512]{2,1,0:T(8,128)} %get-tuple-element.16), calls=%async_computation.7 | async-start | bytes 786432 | tf_op jit(solution)/shard_map/all_to_all | solution.py:245
  140.5 3.6 %collective-permute-start.2 = (f32[8,512]{1,0:T(8,128)S(1)}, f32[8,512]{1,0:T(8,128)S(1)}, u32[]{:S(2)}, u32[]{:S(2)}) collective-permute-start(f32[8,512]{1,0:T(8,128)S(1)} %get-tuple-element.21), channel_id=1, source_target_pairs={{0,8},{8,16},{16,24},{24,32},{32,40},{40,48},{48,56},{56,64},{64,7... | collective-permute-start | bytes 49160 | tf_op jit(solution)/shard_map/ppermute | solution.py:235
  146.0 3.4 %collective-permute-done.3.above_ref = f32[8,512]{1,0:T(8,128)S(1)} collective-permute-done((f32[8,512]{1,0:T(8,128)S(1)}, f32[8,512]{1,0:T(8,128)S(1)}, u32[]{:S(2)}, u32[]{:S(2)}) %collective-permute-start.3) | collective-permute-done | bytes 16416 | tf_op jit(solution)/shard_map/ppermute | solution.py:236
  150.8 2.8 %copy-done.4 = f32[2,3,8,64,421]{4,3,2,1,0:T(8,128)S(1)} copy-done((f32[2,3,8,64,421]{4,3,2,1,0:T(8,128)S(1)}, f32[2,3,8,64,421]{4,3,2,1,0:T(8,128)}, u32[]{:S(2)}) %copy-start.4) | copy-done | bytes 5173272
  153.6 2.3 %shard_map.76 = (f32[32,8,128]{2,1,0:T(8,128)S(1)}, f32[24,512]{1,0:T(8,128)S(1)}) custom-call(f32[8,24,512]{2,1,0:T(8,128)S(1)} %all-to-all-done.7.parts_ref, f32[24,512]{1,0:T(8,128)S(1)} %get-tuple-element.14.s_ref, f32[8,512]{1,0:T(8,128)S(1)} %collective-permute-done.2.below_ref, f32[8,512]{1,0:T(8,128)S(1)} %collective-permute-done.3.above_ref, ...), custom_call_target="tpu_custom_call" | custom-call | tf_op jit(solution)/shard_map/pallas_call | solution.py:243
  155.9 12.8 %all_to_all.55.parts_ref = f32[32,8,128]{2,1,0:T(8,128)S(1)} all-to-all(f32[32,8,128]{2,1,0:T(8,128)S(1)} %get-tuple-element.18), channel_id=1, replica_groups=mesh['param'=32,'sensor'=8] {'param'}, dimensions={0} | all-to-all | bytes 262144 | tf_op jit(solution)/shard_map/all_to_all | solution.py:247
  169.0 21.2 %all_to_all.56.sums_ref = f32[256,1,128]{2,1,0:T(1,128)S(1)} all-to-all(f32[256,1,128]{2,1,0:T(1,128)S(1)} %shard_map.77), channel_id=1, replica_groups=mesh['param'=32,'sensor'=8] {'param','sensor'}, dimensions={0} | all-to-all | bytes 262144 | tf_op jit(solution)/shard_map/all_to_all | solution.py:249
  (34 shorter events, 14.3 us)
Async XLA Ops:
  1.4 2.8 %copy-start = (f32[2,3,8,64,421]{4,3,2,1,0:T(8,128)S(1)}, f32[2,3,8,64,421]{4,3,2,1,0:T(8,128)}, u32[]{:S(2)}) copy-start(f32[2,3,8,64,421]{4,3,2,1,0:T(8,128)} %k_ref.11) | copy-start | bytes 15519748
  4.2 1.2 copy-start.5
  5.4 1.2 copy-start.7
  6.7 14.3 %copy-start.10 = (f32[64,420]{1,0:T(8,128)S(1)}, f32[64,420]{1,0:T(8,128)}, u32[]{:S(2)}) copy-start(f32[64,420]{1,0:T(8,128)} %param.6) | copy-start | bytes 322564
  6.7 36.1 %copy-start.6 = (bf16[512,1024]{1,0:T(8,128)(2,1)S(1)}, bf16[512,1024]{1,0:T(8,128)(2,1)}, u32[]{:S(2)}) copy-start(bf16[512,1024]{1,0:T(8,128)(2,1)} %constant.47.clone.high_ref) | copy-start | bytes 3145732
  6.7 36.1 %copy-start.8 = (bf16[512,1024]{1,0:T(8,128)(2,1)S(1)}, bf16[512,1024]{1,0:T(8,128)(2,1)}, u32[]{:S(2)}) copy-start(bf16[512,1024]{1,0:T(8,128)(2,1)} %constant.48.clone.low_ref) | copy-start | bytes 3145732
  9.7 45.6 %copy-start.9 = (f32[3,8,420]{2,1,0:T(8,128)S(1)}, f32[3,8,420]{2,1,0:T(8,128)}, u32[]{:S(2)}) copy-start(f32[3,8,420]{2,1,0:T(8,128)} %param.7) | copy-start | bytes 120964
  9.7 20.5 %all-to-all-start = ((f32[32,8,128]{2,1,0:T(8,128)}), f32[32,8,128]{2,1,0:T(8,128)S(1)}, u32[]{:S(2)}, u32[]{:S(2)}) async-start(f32[32,8,128]{2,1,0:T(8,128)} %shard_map.68), calls=%async_computation | async-start | bytes 262144 | tf_op jit(solution)/shard_map/all_to_all | solution.py:237
  42.8 2.8 %copy-start.1 = (f32[2,3,8,64,421]{4,3,2,1,0:T(8,128)S(1)}, f32[2,3,8,64,421]{4,3,2,1,0:T(8,128)}, u32[]{:S(2)}) copy-start(f32[2,3,8,64,421]{4,3,2,1,0:T(8,128)} %k_ref.11) | copy-start | bytes 15519748
  48.9 16.7 %all-to-all-start.2 = ((f32[8,24,512]{2,1,0:T(8,128)}), f32[8,24,512]{2,1,0:T(8,128)S(1)}, u32[]{:S(2)}, u32[]{:S(2)}) async-start(f32[8,24,512]{2,1,0:T(8,128)} %get-tuple-element.11), calls=%async_computation.2 | async-start | bytes 786432 | tf_op jit(solution)/shard_map/all_to_all | solution.py:245
  55.3 5.2 %collective-permute-start = (f32[8,512]{1,0:T(8,128)S(1)}, f32[8,512]{1,0:T(8,128)S(1)}, u32[]{:S(2)}, u32[]{:S(2)}) collective-permute-start(f32[8,512]{1,0:T(8,128)S(1)} %get-tuple-element.23), channel_id=1, source_target_pairs={{0,8},{8,16},{16,24},{24,32},{32,40},{40,48},{48,56},{56,64},{64,7... | collective-permute-start | bytes 49160 | tf_op jit(solution)/shard_map/ppermute | solution.py:235
  58.5 5.4 %collective-permute-start.1 = (f32[8,512]{1,0:T(8,128)S(1)}, f32[8,512]{1,0:T(8,128)S(1)}, u32[]{:S(2)}, u32[]{:S(2)}) collective-permute-start(f32[8,512]{1,0:T(8,128)S(1)} %get-tuple-element.22), channel_id=1, source_target_pairs={{8,0},{16,8},{24,16},{32,24},{40,32},{48,40},{56,48},{64,56},{72,6... | collective-permute-start | bytes 49160 | tf_op jit(solution)/shard_map/ppermute | solution.py:236
  65.6 2.8 %copy-start.2 = (f32[2,3,8,64,421]{4,3,2,1,0:T(8,128)S(1)}, f32[2,3,8,64,421]{4,3,2,1,0:T(8,128)}, u32[]{:S(2)}) copy-start(f32[2,3,8,64,421]{4,3,2,1,0:T(8,128)} %k_ref.11) | copy-start | bytes 15519748
  68.4 36.9 %copy-start.3 = (f32[2,3,8,64,421]{4,3,2,1,0:T(8,128)S(1)}, f32[2,3,8,64,421]{4,3,2,1,0:T(8,128)}, u32[]{:S(2)}) copy-start(f32[2,3,8,64,421]{4,3,2,1,0:T(8,128)} %k_ref.11) | copy-start | bytes 15519748
  137.0 13.8 %all-to-all-start.7 = ((f32[8,24,512]{2,1,0:T(8,128)}), f32[8,24,512]{2,1,0:T(8,128)S(1)}, u32[]{:S(2)}, u32[]{:S(2)}) async-start(f32[8,24,512]{2,1,0:T(8,128)} %get-tuple-element.16), calls=%async_computation.7 | async-start | bytes 786432 | tf_op jit(solution)/shard_map/all_to_all | solution.py:245
  140.5 5.5 %collective-permute-start.2 = (f32[8,512]{1,0:T(8,128)S(1)}, f32[8,512]{1,0:T(8,128)S(1)}, u32[]{:S(2)}, u32[]{:S(2)}) collective-permute-start(f32[8,512]{1,0:T(8,128)S(1)} %get-tuple-element.21), channel_id=1, source_target_pairs={{0,8},{8,16},{16,24},{24,32},{32,40},{40,48},{48,56},{56,64},{64,7... | collective-permute-start | bytes 49160 | tf_op jit(solution)/shard_map/ppermute | solution.py:235
  144.1 5.4 %collective-permute-start.3 = (f32[8,512]{1,0:T(8,128)S(1)}, f32[8,512]{1,0:T(8,128)S(1)}, u32[]{:S(2)}, u32[]{:S(2)}) collective-permute-start(f32[8,512]{1,0:T(8,128)S(1)} %get-tuple-element.20), channel_id=1, source_target_pairs={{8,0},{16,8},{24,16},{32,24},{40,32},{48,40},{56,48},{64,56},{72,6... | collective-permute-start | bytes 49160 | tf_op jit(solution)/shard_map/ppermute | solution.py:236
  150.8 2.8 %copy-start.4 = (f32[2,3,8,64,421]{4,3,2,1,0:T(8,128)S(1)}, f32[2,3,8,64,421]{4,3,2,1,0:T(8,128)}, u32[]{:S(2)}) copy-start(f32[2,3,8,64,421]{4,3,2,1,0:T(8,128)} %k_ref.11) | copy-start | bytes 15519748

commit v2 on v1

v2 whole, which is shorter than its diff:
```python
import functools
import math

import jax
import jax.numpy as jnp
import numpy as np
from jax import lax
from jax.experimental import pallas as pl
from jax.experimental.pallas import tpu as pltpu
from jax.sharding import PartitionSpec as P

ITERS = 2
LAMBDA_REG = 0.5
TINY_TERM = 1e-06
LANES = 128
ROWS = 8
F32 = jnp.float32
BF16 = jnp.bfloat16
VMEM_LIMIT = 20 * 1024 * 1024


def dft_table(steps, freqs, pad):
    index = np.arange(pad, dtype=np.int64)
    phase = (index[:, None] * index[None, :]) % (2 * steps)
    angle = phase * (math.pi / steps)
    inside = (index[:, None] < freqs) & (index[None, :] < freqs)
    whole = np.concatenate(
        [np.where(inside, np.cos(angle), 0.0), np.where(inside, -np.sin(angle), 0.0)], axis=1
    )
    high = whole.astype(np.float32).astype(BF16)
    low = (whole - high.astype(np.float64)).astype(np.float32).astype(BF16)
    return high, low


def product(x, high_ref, low_ref, columns):
    rows = x.shape[0]
    high = x.astype(BF16).astype(F32)
    terms = jnp.concatenate([high, x - high], axis=0).astype(BF16)
    dot = functools.partial(jnp.dot, preferred_element_type=F32)
    main = dot(terms, high_ref[:, columns])
    return main[:rows] + main[rows:] + dot(high.astype(BF16), low_ref[:, columns])


def to_series(real_part, imag_part, high_ref, low_ref, steps):
    pad = real_part.shape[1]
    column = lax.broadcasted_iota(jnp.int32, (1, pad), 1)
    weight = jnp.where((column == 0) | (column == steps), 1.0, 2.0) / (2.0 * steps)
    out = product(real_part * weight, high_ref, low_ref, slice(0, pad))
    out += product(imag_part * weight, high_ref, low_ref, slice(pad, 2 * pad))
    return jnp.where(column < steps, out, 0.0)


def lane_blocks(freqs):
    return [(start, min(LANES, freqs - start)) for start in range(0, freqs, LANES)]


def column_copy(c, k_any, k_ref, sems):
    return pltpu.make_async_copy(k_any.at[:, c], k_ref.at[:, c], sems.at[c])


def start_columns(k_any, k_ref, sems):
    for c in range(k_ref.shape[1] if sems is not None else 0):
        column_copy(c, k_any, k_ref, sems).start()


def forward_map(field, k_any, high_ref, low_ref, out_ref, xs_ref, ys_ref, k_ref, sems, steps):
    _, cols, dips, sensors, freqs = k_ref.shape
    pad = field.shape[1]
    xs_ref[...] = product(field, high_ref, low_ref, slice(0, 2 * pad)).reshape(cols, dips, 2 * pad)
    ys_ref[...] = jnp.zeros_like(ys_ref)
    height = min(32, sensors)

    def column(c, carry):
        if sems is not None:
            column_copy(c, k_any, k_ref, sems).wait()
        for start, width in lane_blocks(freqs):
            for top in range(0, sensors, height):
                rows = slice(top, top + height)
                rr = ys_ref[rows, start : start + width]
                ri = ys_ref[rows, pad + start : pad + start + width]
                ii = ir = jnp.zeros((height, width), F32)
                for d in range(dips):
                    kr = k_ref[0, c, d, rows, start : start + width]
                    ki = k_ref[1, c, d, rows, start : start + width]
                    xr = xs_ref[c, d : d + 1, start : start + width]
                    xi = xs_ref[c, d : d + 1, pad + start : pad + start + width]
                    rr = rr + kr * xr
                    ii = ii + ki * xi
                    ri = ri + kr * xi
                    ir = ir + ki * xr
                ys_ref[rows, start : start + width] = rr - ii
                ys_ref[rows, pad + start : pad + start + width] = ri + ir
        return carry

    lax.fori_loop(0, cols, column, 0)
    series = to_series(ys_ref[:, :pad], ys_ref[:, pad:], high_ref, low_ref, steps)
    tiles = pad // LANES
    for o in range(sensors // ROWS):
        for t in range(tiles):
            out_ref[o * tiles + t] = series[o * ROWS : (o + 1) * ROWS, t * LANES : (t + 1) * LANES]


def store_edges(field, dips, inner_ref, outer_ref):
    even = lax.axis_index("param") % 2 == 0
    first, last = field[:dips], field[field.shape[0] - dips :]
    inner_ref[...] = jnp.where(even, last, first)
    outer_ref[...] = jnp.where(even, first, last)


def first_kernel(
    steps,
    s_any,
    k_any,
    high_any,
    low_any,
    out_ref,
    padded_ref,
    inner_ref,
    outer_ref,
    xs_ref,
    ys_ref,
    k_ref,
    sems,
    high_ref,
    low_ref,
    s_ref,
    table_sems,
):
    tables = [
        pltpu.make_async_copy(high_any, high_ref, table_sems.at[0]),
        pltpu.make_async_copy(low_any, low_ref, table_sems.at[1]),
    ]
    initial = pltpu.make_async_copy(s_any, s_ref, table_sems.at[2])
    initial.start()
    for copy in tables:
        copy.start()
    start_columns(k_any, k_ref, sems)
    cols, dips, _ = s_ref.shape
    padded_ref[...] = jnp.zeros_like(padded_ref)
    initial.wait()
    for c in range(cols):
        padded_ref[c * dips : (c + 1) * dips, :steps] = s_ref[c]
    store_edges(padded_ref[...], dips, inner_ref, outer_ref)
    for copy in tables:
        copy.wait()
    forward_map(padded_ref[...], k_any, high_ref, low_ref, out_ref, xs_ref, ys_ref, k_ref, sems, steps)


def stepped(s_ref, g_ref, sums_ref):
    sums = jnp.sum(sums_ref[...], axis=0)
    image_sq = sums[:, :1]
    grad_sq = sums[:, LANES // 2 : LANES // 2 + 1]
    alpha = grad_sq / (image_sq + 8.0 * LAMBDA_REG * grad_sq + TINY_TERM)
    return jnp.maximum(s_ref[...] - alpha * g_ref[...], 0.0)


def step_kernel(s_ref, g_ref, sums_ref, new_ref, inner_ref, outer_ref):
    new = stepped(s_ref, g_ref, sums_ref)
    new_ref[...] = new
    store_edges(new, inner_ref.shape[0], inner_ref, outer_ref)


def map_kernel(steps, s_ref, k_ref, high_ref, low_ref, out_ref, xs_ref, ys_ref):
    forward_map(s_ref[...], None, high_ref, low_ref, out_ref, xs_ref, ys_ref, k_ref, None, steps)


def last_kernel(s_ref, g_ref, sums_ref, out_ref):
    new = stepped(s_ref, g_ref, sums_ref)
    cols, dips, steps = out_ref.shape
    for c in range(cols):
        out_ref[c] = new[c * dips : (c + 1) * dips, :steps]


def misfit_kernel(parts_ref, observed_ref, out_ref, padded_ref):
    steps = observed_ref.shape[1]
    tiles = padded_ref.shape[1] // LANES
    me = lax.axis_index("param")
    padded_ref[...] = jnp.zeros_like(padded_ref)
    padded_ref[:, :steps] = observed_ref[pl.ds(pl.multiple_of(me // tiles * ROWS, ROWS), ROWS), :]
    misfit = jnp.sum(parts_ref[...], axis=0)
    for t in range(tiles):
        misfit -= jnp.where(me % tiles == t, padded_ref[:, t * LANES : (t + 1) * LANES], 0.0)
    out_ref[...] = jnp.broadcast_to(misfit[None], out_ref.shape)


def packed(series, cols, steps):
    whole = steps // LANES
    width = steps - whole * LANES
    tiles = []
    tail = None
    for c in range(cols):
        rows = series[c * ROWS : (c + 1) * ROWS]
        tiles += [rows[:, t * LANES : (t + 1) * LANES] for t in range(whole)]
        end = rows[:, whole * LANES :]
        tail = end if tail is None else tail + pltpu.roll(end, c * width, 1)
    return tiles + [tail]


def unpacked(tiles, cols, steps):
    whole = steps // LANES
    width = steps - whole * LANES
    lane = lax.broadcasted_iota(jnp.int32, (ROWS, LANES), 1)
    tail = tiles[cols * whole]
    rows = []
    for c in range(cols):
        end = pltpu.roll(tail, LANES - c * width, 1) if c else tail
        parts = [tiles[c * whole + t] for t in range(whole)] + [jnp.where(lane < width, end, 0.0)]
        rows.append(jnp.concatenate(parts, axis=1))
    return jnp.concatenate(rows, axis=0)


def adjoint_kernel(steps, r_ref, k_ref, high_ref, low_ref, out_ref, res_ref, xs_ref, ys_ref):
    _, cols, dips, sensors, freqs = k_ref.shape
    pad = xs_ref.shape[2] // 2
    tiles = pad // LANES
    rows = [
        jnp.concatenate([r_ref[o * tiles + t] for t in range(tiles)], axis=1)
        for o in range(sensors // ROWS)
    ]
    misfit = jnp.concatenate(rows, axis=0)
    res_ref[...] = misfit[:, :steps]
    ys_ref[...] = product(misfit, high_ref, low_ref, slice(0, 2 * pad))
    xs_ref[...] = jnp.zeros_like(xs_ref)

    def column(c, carry):
        for start, width in lane_blocks(freqs):
            rr = [ys_ref[top : top + ROWS, start : start + width] for top in range(0, sensors, ROWS)]
            ri = [ys_ref[top : top + ROWS, pad + start : pad + start + width] for top in range(0, sensors, ROWS)]
            for d in range(dips):
                real = jnp.zeros((ROWS, width), F32)
                imag = jnp.zeros((ROWS, width), F32)
                for i in range(sensors // ROWS):
                    kr = k_ref[0, c, d, i * ROWS : (i + 1) * ROWS, start : start + width]
                    ki = k_ref[1, c, d, i * ROWS : (i + 1) * ROWS, start : start + width]
                    real = real + (kr * rr[i] + ki * ri[i])
                    imag = imag + (kr * ri[i] - ki * rr[i])
                xs_ref[c, d : d + 1, start : start + width] = jnp.sum(real, axis=0, keepdims=True)
                xs_ref[c, d : d + 1, pad + start : pad + start + width] = jnp.sum(imag, axis=0, keepdims=True)
        return carry

    lax.fori_loop(0, cols, column, 0)
    spectra = xs_ref[...].reshape(cols * dips, 2 * pad)
    series = to_series(spectra[:, :pad], spectra[:, pad:], high_ref, low_ref, steps)
    for j, tile in enumerate(packed(series, cols, steps)):
        for i in range(out_ref.shape[0]):
            out_ref[i, j] = tile


def gradient_kernel(
    steps, parts_ref, s_ref, inner_ref, outer_ref, k_ref, high_ref, low_ref, out_ref, g_ref, xs_ref, ys_ref
):
    cols, dips = k_ref.shape[1:3]
    field = s_ref[...]
    count = cols * dips
    even = lax.axis_index("param") % 2 == 0
    inner, outer = inner_ref[...], outer_ref[...]
    below, above = jnp.where(even, outer, inner), jnp.where(even, inner, outer)
    earlier = jnp.concatenate([below, field[: count - dips]], axis=0)
    later = jnp.concatenate([field[dips:], above], axis=0)
    dip = lax.broadcasted_iota(jnp.int32, field.shape, 0) % dips
    upper = jnp.where(dip == 0, 0.0, pltpu.roll(field, 1, 0))
    lower = jnp.where(dip == dips - 1, 0.0, pltpu.roll(field, count - 1, 0))
    smooth = 4.0 * field - (earlier + later) - lower - upper
    summed = jnp.sum(parts_ref[...], axis=0)
    back = unpacked([summed[j] for j in range(summed.shape[0])], cols, steps)
    gradient = back + LAMBDA_REG * smooth
    g_ref[...] = gradient
    forward_map(gradient, None, high_ref, low_ref, out_ref, xs_ref, ys_ref, k_ref, None, steps)


def squares_kernel(copies, parts_ref, g_ref, out_ref):
    image = jnp.sum(parts_ref[...], axis=0)
    gradient = g_ref[...]
    image_sq = jnp.sum(image * image, keepdims=True)
    grad_sq = jnp.sum(gradient * gradient, keepdims=True) * (1.0 / copies)
    lane = lax.broadcasted_iota(jnp.int32, (1, LANES), 1)
    both = jnp.where(lane < LANES // 2, image_sq, grad_sq)
    out_ref[...] = jnp.broadcast_to(both[None], out_ref.shape)


def shape(*dims):
    return jax.ShapeDtypeStruct(dims, F32)


def call(kernel, out_shape, scratch=(), outside=(), inputs=0):
    specs = [pl.BlockSpec(memory_space=pltpu.HBM if i in outside else pltpu.VMEM) for i in range(inputs)]
    return pl.pallas_call(
        kernel,
        out_shape=out_shape,
        scratch_shapes=[pltpu.VMEM(dims, F32) if isinstance(dims, tuple) else dims for dims in scratch],
        compiler_params=pltpu.CompilerParams(vmem_limit_bytes=VMEM_LIMIT),
        **({"in_specs": specs} if inputs else {}),
    )


def body(kernel_spec, observed, initial):
    _, cols, dips, sensors, freqs = kernel_spec.shape
    steps = observed.shape[1]
    points = cols * dips
    pad = -(-freqs // LANES) * LANES
    tiles = pad // LANES
    params = lax.axis_size("param")
    groups = lax.axis_size("sensor")
    assert params == sensors // ROWS * tiles and dips == ROWS
    assert cols * (steps % LANES) <= LANES
    high, low = (jnp.asarray(part) for part in dft_table(steps, freqs, pad))
    tiled = shape(params, ROWS, LANES)
    field = shape(points, pad)
    work = [(cols, dips, 2 * pad), (sensors, 2 * pad), kernel_spec.shape, pltpu.SemaphoreType.DMA((cols,))]
    table = pltpu.VMEM(high.shape, BF16)
    swap = functools.partial(lax.all_to_all, split_axis=0, concat_axis=0)
    stay = functools.partial(pltpu.with_memory_space_constraint, memory_space=pltpu.HBM)
    spec = stay(kernel_spec)
    pairs = [(i, i ^ 1) for i in range(params)]
    others = [(i, i + 1 if i % 2 else i - 1) for i in range(1, params - 1)]
    edge = shape(dips, pad)
    map_work = work[:2]

    for iteration in range(ITERS):
        if iteration == 0:
            parts, sources, inner, outer = call(
                functools.partial(first_kernel, steps),
                (tiled, field, edge, edge),
                work + [table, table, pltpu.VMEM(initial.shape, F32), pltpu.SemaphoreType.DMA((3,))],
                outside=(0, 1, 2, 3),
                inputs=4,
            )(stay(initial), spec, stay(high), stay(low))
        else:
            sources, inner, outer = call(step_kernel, (field, edge, edge))(sources, gradient, sums)
            parts = call(functools.partial(map_kernel, steps), tiled, map_work)(
                sources, kernel_spec, high, low
            )
        inner, outer = lax.ppermute(inner, "param", pairs), lax.ppermute(outer, "param", others)
        if iteration == 0:
            parts, inner, outer = lax.optimization_barrier((swap(parts, "param"), inner, outer))
        else:
            parts, inner, outer = lax.optimization_barrier((parts, inner, outer))
            parts = swap(parts, "param")
        misfit = call(misfit_kernel, tiled, [(ROWS, pad)])(parts, observed)
        count = cols * (steps // LANES) + 1
        partial, residual = call(
            functools.partial(adjoint_kernel, steps),
            (shape(groups, count, ROWS, LANES), shape(sensors, steps)),
            map_work,
        )(swap(misfit, "param"), kernel_spec, high, low)
        image, gradient = call(functools.partial(gradient_kernel, steps), (tiled, field), map_work)(
            swap(partial, "sensor"), sources, inner, outer, kernel_spec, high, low
        )
        squares = call(functools.partial(squares_kernel, groups), shape(params * groups, 1, LANES))(
            swap(image, "param"), gradient
        )
        sums = swap(squares, ("param", "sensor"))
    sources = call(last_kernel, shape(cols, dips, steps))(sources, gradient, sums)
    return (sources, residual)


def solution(mesh):
    placed = (P(None, "param", None, "sensor", None), P("sensor", None), P("param", None, None))
    return jax.shard_map(
        body,
        mesh=mesh,
        in_specs=placed,
        out_specs=(P("param", None, None), P("sensor", None)),
        check_vma=False,
    )
```

time: 192 us -> 180 us (0.938)
  blocking collectives: 106 us -> 132 us
  starting transfers between devices: 31.7 us -> 18.1 us
  waiting for transfers between devices: 19.1 us -> 6.14 us
  local copies, waits for them, and re-layouts: 14.4 us -> 2.81 us
    all_to_all x1 -> x3, blocking collectives: 13 us -> 41.9 us  [the longest x2 28.1 us: body(): swap(partial, 'sensor')]
    unnamed x22 -> x12, local copies, waits for them, and re-layouts: 13.6 us -> 2.81 us
    all_to_all x3 -> x1, starting transfers between devices: 21.1 us -> 11.1 us  [body(): swap(parts, 'param')]
    all_to_all x3 -> x1, waiting for transfers between devices: 12.3 us -> 3.43 us  [body(): swap(parts, 'param')]
    all_to_all x2, blocking collectives: 42.7 us -> 36.3 us  [body(): sums = swap(squares, ('param', 'sensor'))]
    ppermute x4, waiting for transfers between devices: 6.83 us -> 2.71 us  [the longest x2 2.7 us: body(): lax.ppermute(outer, 'param', others)]
    ppermute x4, starting transfers between devices: 10.6 us -> 7 us  [the longest x2 5.61 us: body(): lax.ppermute(outer, 'param', others)]
    all_to_all x2, blocking collectives: 25 us -> 27.1 us  [body(): swap(misfit, 'param')]
  transfers between devices with their start and end apart: 7 -> 5, of which waited for: 5 -> 3; matrix products, arithmetic and copies ran while one was open for 0% -> 0% of each run, Pallas kernels for 0% -> 1%
where the time goes in v2:
time: 180 us; the launch traced here: 179 us
  blocking collectives  132 us (73%)
  Pallas kernels  19.5 us (11%)
  starting transfers between devices  18.1 us (10%)
  waiting for transfers between devices  6.14 us (3%)
  local copies, waits for them, and re-layouts  2.81 us (2%)
    all_to_all x2, blocking collectives, body(): sums = swap(squares, ('param', 'sensor'))  36.3 us
    all_to_all x2, blocking collectives, body(): swap(partial, 'sensor')  28.1 us
    all_to_all x2, blocking collectives, body(): swap(misfit, 'param')  27.1 us
    all_to_all x2, blocking collectives, body(): swap(image, 'param')  26.4 us
    all_to_all x1, blocking collectives, body(): parts = swap(parts, 'param')  13.8 us
    all_to_all x1, starting transfers between devices, body(): swap(parts, 'param')  11.1 us
    pallas_call x1, Pallas kernels, body(): call(functools.partial(first_kernel, steps), (tiled, field, edge, edge),...  6.04 us
    ppermute x2, starting transfers between devices, body(): lax.ppermute(outer, 'param', others)  5.61 us
  transfers between devices with their start and end apart: 5, of which 3 were waited for; matrix products, arithmetic and copies ran while one was open for 0% of the time, Pallas kernels for 1%

profile of v2, /device:TPU:1, one launch (start us, length us, event | category | flops | bytes accessed | tf_op | source)
XLA Modules:
  0.0 179.0 jit_solution(14317296035236289977)
XLA Ops:
  0.7 6.0 %shard_map.68 = (f32[32,8,128]{2,1,0:T(8,128)}, f32[24,512]{1,0:T(8,128)S(1)}, f32[8,512]{1,0:T(8,128)S(1)}, f32[8,512]{1,0:T(8,128)S(1)}) custom-call(f32[3,8,420]{2,1,0:T(8,128)} %s_any.1, f32[2,3,8,64,421]{4,3,2,1,0:T(8,128)} %k_ref.9, bf16[512,1024]{1,0:T(8,128)(2,1)} %constant.4.clone.high_any.high_ref, bf16[512,1024]{1,0:T(8,128)(2,1)} %constant.5.clone.low_any.low_ref), custom_call_target="tpu_custom_call" | custom-call | tf_op jit(solution)/shard_map/pallas_call | solution.py:321
  6.7 11.1 %all-to-all-start = ((f32[32,8,128]{2,1,0:T(8,128)}), f32[32,8,128]{2,1,0:T(8,128)S(1)}, u32[]{:S(2)}, u32[]{:S(2)}) async-start(f32[32,8,128]{2,1,0:T(8,128)} %get-tuple-element.23), calls=%async_computation | async-start | bytes 262144 | tf_op jit(solution)/shard_map/all_to_all | solution.py:335
  18.2 3.4 %collective-permute-start.1 = (f32[8,512]{1,0:T(8,128)S(1)}, f32[8,512]{1,0:T(8,128)S(1)}, u32[]{:S(2)}, u32[]{:S(2)}) collective-permute-start(f32[8,512]{1,0:T(8,128)S(1)} %get-tuple-element.25), channel_id=1, source_target_pairs={{8,16},{16,8},{24,32},{32,24},{40,48},{48,40},{56,64},{64,56},{72,... | collective-permute-start | bytes 49160 | tf_op jit(solution)/shard_map/ppermute | solution.py:333
  21.6 2.0 %collective-permute-done.1.outer_ref = f32[8,512]{1,0:T(8,128)S(1)} collective-permute-done((f32[8,512]{1,0:T(8,128)S(1)}, f32[8,512]{1,0:T(8,128)S(1)}, u32[]{:S(2)}, u32[]{:S(2)}) %collective-permute-start.1) | collective-permute-done | bytes 16416 | tf_op jit(solution)/shard_map/ppermute | solution.py:333
  23.7 3.4 %all-to-all-done.parts_ref = f32[32,8,128]{2,1,0:T(8,128)S(1)} async-done(((f32[32,8,128]{2,1,0:T(8,128)}), f32[32,8,128]{2,1,0:T(8,128)S(1)}, u32[]{:S(2)}, u32[]{:S(2)}) %all-to-all-start) | async-done | bytes 131104 | tf_op jit(solution)/shard_map/all_to_all | solution.py:335
  27.1 14.5 %all_to_all.50.r_ref = f32[32,8,128]{2,1,0:T(8,128)S(1)} all-to-all(f32[32,8,128]{2,1,0:T(8,128)S(1)} %shard_map.69), channel_id=1, replica_groups=mesh['param'=32,'sensor'=8] {'param'}, dimensions={0} | all-to-all | bytes 262144 | tf_op jit(solution)/shard_map/all_to_all | solution.py:345
  41.7 2.8 %copy-done = f32[2,3,8,64,421]{4,3,2,1,0:T(8,128)S(1)} copy-done((f32[2,3,8,64,421]{4,3,2,1,0:T(8,128)S(1)}, f32[2,3,8,64,421]{4,3,2,1,0:T(8,128)}, u32[]{:S(2)}) %copy-start) | copy-done | bytes 5173272
  44.5 2.4 %shard_map.70 = (f32[8,10,8,128]{3,2,1,0:T(8,128)S(1)}, f32[64,420]{1,0:T(8,128)}) custom-call(f32[32,8,128]{2,1,0:T(8,128)S(1)} %all_to_all.50.r_ref, f32[2,3,8,64,421]{4,3,2,1,0:T(8,128)S(1)} %copy-done, bf16[512,1024]{1,0:T(8,128)(2,1)S(1)} %copy-done.2, bf16[512,1024]{1,0:T(8,128)(2,1)S(1)} %copy-done.1), custom_call_target="tpu_custom_call" | custom-call | tf_op jit(solution)/shard_map/pallas_call | solution.py:341
  46.9 15.5 %all_to_all.51.parts_ref = f32[8,10,8,128]{3,2,1,0:T(8,128)S(1)} all-to-all(f32[8,10,8,128]{3,2,1,0:T(8,128)S(1)} %get-tuple-element.27), channel_id=1, replica_groups=mesh['param'=32,'sensor'=8] {'sensor'}, dimensions={0} | all-to-all | bytes 655360 | tf_op jit(solution)/shard_map/all_to_all | solution.py:347
  62.5 2.1 %shard_map.71 = (f32[32,8,128]{2,1,0:T(8,128)S(1)}, f32[24,512]{1,0:T(8,128)S(1)}) custom-call(f32[8,10,8,128]{3,2,1,0:T(8,128)S(1)} %all_to_all.51.parts_ref, f32[24,512]{1,0:T(8,128)S(1)} %get-tuple-element.22.s_ref, f32[8,512]{1,0:T(8,128)S(1)} %collective-permute-done.inner_ref, f32[8,512]{1,0:T(8,128)S(1)} %collective-permute-done.1.outer_ref, ...), custom_call_target="tpu_custom_call" | custom-call | tf_op jit(solution)/shard_map/pallas_call | solution.py:346
  64.6 13.2 %all_to_all.52.parts_ref = f32[32,8,128]{2,1,0:T(8,128)S(1)} all-to-all(f32[32,8,128]{2,1,0:T(8,128)S(1)} %get-tuple-element.31), channel_id=1, replica_groups=mesh['param'=32,'sensor'=8] {'param'}, dimensions={0} | all-to-all | bytes 262144 | tf_op jit(solution)/shard_map/all_to_all | solution.py:350
  78.0 18.1 %all_to_all.53.sums_ref = f32[256,1,128]{2,1,0:T(1,128)S(1)} all-to-all(f32[256,1,128]{2,1,0:T(1,128)S(1)} %shard_map.72), channel_id=1, replica_groups=mesh['param'=32,'sensor'=8] {'param','sensor'}, dimensions={0} | all-to-all | bytes 262144 | tf_op jit(solution)/shard_map/all_to_all | solution.py:352
  96.7 1.1 collective-permute-start.2
  97.8 2.2 %collective-permute-start.3 = (f32[8,512]{1,0:T(8,128)S(1)}, f32[8,512]{1,0:T(8,128)S(1)}, u32[]{:S(2)}, u32[]{:S(2)}) collective-permute-start(f32[8,512]{1,0:T(8,128)S(1)} %get-tuple-element.34), channel_id=1, source_target_pairs={{8,16},{16,8},{24,32},{32,24},{40,48},{48,40},{56,64},{64,56},{72,... | collective-permute-start | bytes 49160 | tf_op jit(solution)/shard_map/ppermute | solution.py:333
  100.0 2.1 %shard_map.74 = f32[32,8,128]{2,1,0:T(8,128)S(1)} custom-call(f32[24,512]{1,0:T(8,128)S(1)} %get-tuple-element.32.s_ref, f32[2,3,8,64,421]{4,3,2,1,0:T(8,128)S(1)} %bitcast.1, bf16[512,1024]{1,0:T(8,128)(2,1)S(1)} %copy-done.2, bf16[512,1024]{1,0:T(8,128)(2,1)S(1)} %copy-done.1), custom_call_target="tpu_custom_call" | custom-call | tf_op jit(solution)/shard_map/pallas_call | solution.py:330
  102.2 0.7 collective-permute-done.3.outer_ref
  102.8 13.8 %all_to_all.54.parts_ref = f32[32,8,128]{2,1,0:T(8,128)S(1)} all-to-all(f32[32,8,128]{2,1,0:T(8,128)S(1)} %shard_map.74), channel_id=1, replica_groups=mesh['param'=32,'sensor'=8] {'param'}, dimensions={0} | all-to-all | bytes 262144 | tf_op jit(solution)/shard_map/all_to_all | solution.py:338
  116.6 12.5 %all_to_all.55.r_ref = f32[32,8,128]{2,1,0:T(8,128)S(1)} all-to-all(f32[32,8,128]{2,1,0:T(8,128)S(1)} %shard_map.75), channel_id=1, replica_groups=mesh['param'=32,'sensor'=8] {'param'}, dimensions={0} | all-to-all | bytes 262144 | tf_op jit(solution)/shard_map/all_to_all | solution.py:345
  129.2 2.4 %shard_map.76 = (f32[8,10,8,128]{3,2,1,0:T(8,128)S(1)}, f32[64,420]{1,0:T(8,128)}) custom-call(f32[32,8,128]{2,1,0:T(8,128)S(1)} %all_to_all.55.r_ref, f32[2,3,8,64,421]{4,3,2,1,0:T(8,128)S(1)} %bitcast.1, bf16[512,1024]{1,0:T(8,128)(2,1)S(1)} %copy-done.2, bf16[512,1024]{1,0:T(8,128)(2,1)S(1)} %copy-done.1), custom_call_target="tpu_custom_call" | custom-call | tf_op jit(solution)/shard_map/pallas_call | solution.py:341
  131.6 12.6 %all_to_all.56.parts_ref = f32[8,10,8,128]{3,2,1,0:T(8,128)S(1)} all-to-all(f32[8,10,8,128]{3,2,1,0:T(8,128)S(1)} %get-tuple-element.36), channel_id=1, replica_groups=mesh['param'=32,'sensor'=8] {'sensor'}, dimensions={0} | all-to-all | bytes 655360 | tf_op jit(solution)/shard_map/all_to_all | solution.py:347
  144.2 2.1 %shard_map.77 = (f32[32,8,128]{2,1,0:T(8,128)S(1)}, f32[24,512]{1,0:T(8,128)S(1)}) custom-call(f32[8,10,8,128]{3,2,1,0:T(8,128)S(1)} %all_to_all.56.parts_ref, f32[24,512]{1,0:T(8,128)S(1)} %get-tuple-element.32.s_ref, f32[8,512]{1,0:T(8,128)S(1)} %collective-permute-done.2.inner_ref, f32[8,512]{1,0:T(8,128)S(1)} %collective-permute-done.3.outer_ref, ...), custom_call_target="tpu_custom_call" | custom-call | tf_op jit(solution)/shard_map/pallas_call | solution.py:346
  146.3 13.2 %all_to_all.57.parts_ref = f32[32,8,128]{2,1,0:T(8,128)S(1)} all-to-all(f32[32,8,128]{2,1,0:T(8,128)S(1)} %get-tuple-element.40), channel_id=1, replica_groups=mesh['param'=32,'sensor'=8] {'param'}, dimensions={0} | all-to-all | bytes 262144 | tf_op jit(solution)/shard_map/all_to_all | solution.py:350
  159.8 18.1 %all_to_all.58.sums_ref = f32[256,1,128]{2,1,0:T(1,128)S(1)} all-to-all(f32[256,1,128]{2,1,0:T(1,128)S(1)} %shard_map.78), channel_id=1, replica_groups=mesh['param'=32,'sensor'=8] {'param','sensor'}, dimensions={0} | all-to-all | bytes 262144 | tf_op jit(solution)/shard_map/all_to_all | solution.py:352
  177.9 1.1 shard_map.79
  (20 shorter events, 1.4 us)
Async XLA Ops:
  0.6 41.0 %copy-start.1 = (bf16[512,1024]{1,0:T(8,128)(2,1)S(1)}, bf16[512,1024]{1,0:T(8,128)(2,1)}, u32[]{:S(2)}) copy-start(bf16[512,1024]{1,0:T(8,128)(2,1)} %constant.5.clone.low_any.low_ref) | copy-start | bytes 3145732
  0.6 41.0 %copy-start.2 = (bf16[512,1024]{1,0:T(8,128)(2,1)S(1)}, bf16[512,1024]{1,0:T(8,128)(2,1)}, u32[]{:S(2)}) copy-start(bf16[512,1024]{1,0:T(8,128)(2,1)} %constant.4.clone.high_any.high_ref) | copy-start | bytes 3145732
  0.7 26.4 %copy-start.3 = (f32[64,420]{1,0:T(8,128)S(1)}, f32[64,420]{1,0:T(8,128)}, u32[]{:S(2)}) copy-start(f32[64,420]{1,0:T(8,128)} %observed_ref.3) | copy-start | bytes 322564
  6.7 20.4 %all-to-all-start = ((f32[32,8,128]{2,1,0:T(8,128)}), f32[32,8,128]{2,1,0:T(8,128)S(1)}, u32[]{:S(2)}, u32[]{:S(2)}) async-start(f32[32,8,128]{2,1,0:T(8,128)} %get-tuple-element.23), calls=%async_computation | async-start | bytes 262144 | tf_op jit(solution)/shard_map/all_to_all | solution.py:335
  17.9 3.7 %collective-permute-start = (f32[8,512]{1,0:T(8,128)S(1)}, f32[8,512]{1,0:T(8,128)S(1)}, u32[]{:S(2)}, u32[]{:S(2)}) collective-permute-start(f32[8,512]{1,0:T(8,128)S(1)} %get-tuple-element.24), channel_id=1, source_target_pairs={{0,8},{8,0},{16,24},{24,16},{32,40},{40,32},{48,56},{56,48},{64,72... | collective-permute-start | bytes 49160 | tf_op jit(solution)/shard_map/ppermute | solution.py:333
  18.2 5.5 %collective-permute-start.1 = (f32[8,512]{1,0:T(8,128)S(1)}, f32[8,512]{1,0:T(8,128)S(1)}, u32[]{:S(2)}, u32[]{:S(2)}) collective-permute-start(f32[8,512]{1,0:T(8,128)S(1)} %get-tuple-element.25), channel_id=1, source_target_pairs={{8,16},{16,8},{24,32},{32,24},{40,48},{48,40},{56,64},{64,56},{72,... | collective-permute-start | bytes 49160 | tf_op jit(solution)/shard_map/ppermute | solution.py:333
  41.7 2.8 %copy-start = (f32[2,3,8,64,421]{4,3,2,1,0:T(8,128)S(1)}, f32[2,3,8,64,421]{4,3,2,1,0:T(8,128)}, u32[]{:S(2)}) copy-start(f32[2,3,8,64,421]{4,3,2,1,0:T(8,128)} %k_ref.9) | copy-start | bytes 15519748
  44.5 55.5 %slice-start = ((s8[6291456]{0:T(1024)(128)(4,1)}), s8[4194304]{0:T(1024)(128)(4,1)S(1)}, s32[]{:S(2)}) async-start(s8[6291456]{0:T(1024)(128)(4,1)} %bitcast), calls=%async_computation.10 | async-start | bytes 8388608
  62.5 37.6 %slice-start.1 = ((s8[6291456]{0:T(1024)(128)(4,1)}), s8[2097152]{0:T(1024)(128)(4,1)S(1)}, s32[]{:S(2)}) async-start(s8[6291456]{0:T(1024)(128)(4,1)} %bitcast), calls=%async_computation.11 | async-start | bytes 4194304
  96.7 5.4 %collective-permute-start.2 = (f32[8,512]{1,0:T(8,128)S(1)}, f32[8,512]{1,0:T(8,128)S(1)}, u32[]{:S(2)}, u32[]{:S(2)}) collective-permute-start(f32[8,512]{1,0:T(8,128)S(1)} %get-tuple-element.33), channel_id=1, source_target_pairs={{0,8},{8,0},{16,24},{24,16},{32,40},{40,32},{48,56},{56,48},{64,72... | collective-permute-start | bytes 49160 | tf_op jit(solution)/shard_map/ppermute | solution.py:333
  97.8 5.0 %collective-permute-start.3 = (f32[8,512]{1,0:T(8,128)S(1)}, f32[8,512]{1,0:T(8,128)S(1)}, u32[]{:S(2)}, u32[]{:S(2)}) collective-permute-start(f32[8,512]{1,0:T(8,128)S(1)} %get-tuple-element.34), channel_id=1, source_target_pairs={{8,16},{16,8},{24,32},{32,24},{40,48},{48,40},{56,64},{64,56},{72,... | collective-permute-start | bytes 49160 | tf_op jit(solution)/shard_map/ppermute | solution.py:333

commit v3 on v2

--- a/solution.py
+++ b/solution.py
@@ -117,12 +117,12 @@
     padded_ref,
     inner_ref,
     outer_ref,
+    high_ref,
+    low_ref,
     xs_ref,
     ys_ref,
     k_ref,
     sems,
-    high_ref,
-    low_ref,
     s_ref,
     table_sems,
 ):
@@ -146,26 +146,60 @@
     forward_map(padded_ref[...], k_any, high_ref, low_ref, out_ref, xs_ref, ys_ref, k_ref, sems, steps)
 
 
-def stepped(s_ref, g_ref, sums_ref):
+def step_size(sums_ref):
     sums = jnp.sum(sums_ref[...], axis=0)
     image_sq = sums[:, :1]
-    grad_sq = sums[:, LANES // 2 : LANES // 2 + 1]
-    alpha = grad_sq / (image_sq + 8.0 * LAMBDA_REG * grad_sq + TINY_TERM)
-    return jnp.maximum(s_ref[...] - alpha * g_ref[...], 0.0)
-
-
-def step_kernel(s_ref, g_ref, sums_ref, new_ref, inner_ref, outer_ref):
-    new = stepped(s_ref, g_ref, sums_ref)
+    grad_sq = sums[:, LANES // 4 : LANES // 4 + 1]
+    return grad_sq / (image_sq + 8.0 * LAMBDA_REG * grad_sq + TINY_TERM)
+
+
+def stepped(field, gradient, alpha):
+    return jnp.maximum(field - alpha * gradient, 0.0)
+
+
+def gathered_row(sums_ref, neighbour, exists, groups):
+    lane = lax.broadcasted_iota(jnp.int32, (1, LANES), 1)
+    start = jnp.where(exists, neighbour, 0) * groups
+    tiles = []
+    for i in range(0, groups, 2):
+        low, high = sums_ref[start + i], sums_ref[start + i + 1]
+        tiles.append(jnp.where(lane < LANES // 2, pltpu.roll(low, LANES // 2, 1), high))
+    return jnp.where(exists, jnp.concatenate(tiles, axis=1), 0.0)
+
+
+def step_kernel(
+    steps,
+    params,
+    groups,
+    s_ref,
+    g_ref,
+    sums_ref,
+    inner_ref,
+    outer_ref,
+    k_ref,
+    high_ref,
+    low_ref,
+    out_ref,
+    new_ref,
+    new_inner_ref,
+    new_outer_ref,
+    xs_ref,
+    ys_ref,
+):
+    me = lax.axis_index("param")
+    even = me % 2 == 0
+    alpha = step_size(sums_ref)
+    new = stepped(s_ref[...], g_ref[...], alpha)
     new_ref[...] = new
-    store_edges(new, inner_ref.shape[0], inner_ref, outer_ref)
-
-
-def map_kernel(steps, s_ref, k_ref, high_ref, low_ref, out_ref, xs_ref, ys_ref):
-    forward_map(s_ref[...], None, high_ref, low_ref, out_ref, xs_ref, ys_ref, k_ref, None, steps)
+    below = gathered_row(sums_ref, me - 1, me > 0, groups)
+    above = gathered_row(sums_ref, me + 1, me < params - 1, groups)
+    new_inner_ref[...] = stepped(inner_ref[...], jnp.where(even, above, below), alpha)
+    new_outer_ref[...] = stepped(outer_ref[...], jnp.where(even, below, above), alpha)
+    forward_map(new, None, high_ref, low_ref, out_ref, xs_ref, ys_ref, k_ref, None, steps)
 
 
 def last_kernel(s_ref, g_ref, sums_ref, out_ref):
-    new = stepped(s_ref, g_ref, sums_ref)
+    new = stepped(s_ref[...], g_ref[...], step_size(sums_ref))
     cols, dips, steps = out_ref.shape
     for c in range(cols):
         out_ref[c] = new[c * dips : (c + 1) * dips, :steps]
@@ -209,7 +243,10 @@
     return jnp.concatenate(rows, axis=0)
 
 
-def adjoint_kernel(steps, r_ref, k_ref, high_ref, low_ref, out_ref, res_ref, xs_ref, ys_ref):
+def adjoint_kernel(
+    steps, r_ref, inner_ref, outer_ref, k_ref, high_ref, low_ref, out_ref, res_ref, xs_ref, ys_ref, k_any=None, sems=None
+):
+    start_columns(k_any, k_ref, sems)
     _, cols, dips, sensors, freqs = k_ref.shape
     pad = xs_ref.shape[2] // 2
     tiles = pad // LANES
@@ -223,6 +260,8 @@
     xs_ref[...] = jnp.zeros_like(xs_ref)
 
     def column(c, carry):
+        if sems is not None:
+            column_copy(c, k_any, k_ref, sems).wait()
         for start, width in lane_blocks(freqs):
             rr = [ys_ref[top : top + ROWS, start : start + width] for top in range(0, sensors, ROWS)]
             ri = [ys_ref[top : top + ROWS, pad + start : pad + start + width] for top in range(0, sensors, ROWS)]
@@ -241,22 +280,35 @@
     lax.fori_loop(0, cols, column, 0)
     spectra = xs_ref[...].reshape(cols * dips, 2 * pad)
     series = to_series(spectra[:, :pad], spectra[:, pad:], high_ref, low_ref, steps)
+    even = lax.axis_index("param") % 2 == 0
+    inner, outer = inner_ref[...], outer_ref[...]
+    mine = lax.broadcasted_iota(jnp.int32, inner.shape, 0) == lax.axis_index("sensor")
+    below = jnp.where(mine, jnp.where(even, outer, inner), 0.0)
+    above = jnp.where(mine, jnp.where(even, inner, outer), 0.0)
+    inside = jnp.zeros(((cols - 2) * dips, pad), F32)
+    series -= LAMBDA_REG * jnp.concatenate([below, inside, above], axis=0)
     for j, tile in enumerate(packed(series, cols, steps)):
         for i in range(out_ref.shape[0]):
             out_ref[i, j] = tile
 
 
+def first_adjoint_kernel(
+    steps, r_ref, inner_ref, outer_ref, k_any, high_ref, low_ref, out_ref, res_ref, k_ref, xs_ref, ys_ref, sems
+):
+    adjoint_kernel(
+        steps, r_ref, inner_ref, outer_ref, k_ref, high_ref, low_ref, out_ref, res_ref, xs_ref, ys_ref, k_any, sems
+    )
+
+
 def gradient_kernel(
-    steps, parts_ref, s_ref, inner_ref, outer_ref, k_ref, high_ref, low_ref, out_ref, g_ref, xs_ref, ys_ref
+    steps, parts_ref, s_ref, k_ref, high_ref, low_ref, out_ref, g_ref, xs_ref, ys_ref
 ):
     cols, dips = k_ref.shape[1:3]
     field = s_ref[...]
     count = cols * dips
-    even = lax.axis_index("param") % 2 == 0
-    inner, outer = inner_ref[...], outer_ref[...]
-    below, above = jnp.where(even, outer, inner), jnp.where(even, inner, outer)
-    earlier = jnp.concatenate([below, field[: count - dips]], axis=0)
-    later = jnp.concatenate([field[dips:], above], axis=0)
+    edge = jnp.zeros((dips, field.shape[1]), F32)
+    earlier = jnp.concatenate([edge, field[: count - dips]], axis=0)
+    later = jnp.concatenate([field[dips:], edge], axis=0)
     dip = lax.broadcasted_iota(jnp.int32, field.shape, 0) % dips
     upper = jnp.where(dip == 0, 0.0, pltpu.roll(field, 1, 0))
     lower = jnp.where(dip == dips - 1, 0.0, pltpu.roll(field, count - 1, 0))
@@ -268,14 +320,34 @@
     forward_map(gradient, None, high_ref, low_ref, out_ref, xs_ref, ys_ref, k_ref, None, steps)
 
 
-def squares_kernel(copies, parts_ref, g_ref, out_ref):
+def squares_kernel(params, groups, parts_ref, g_ref, out_ref):
     image = jnp.sum(parts_ref[...], axis=0)
     gradient = g_ref[...]
     image_sq = jnp.sum(image * image, keepdims=True)
-    grad_sq = jnp.sum(gradient * gradient, keepdims=True) * (1.0 / copies)
+    grad_sq = jnp.sum(gradient * gradient, keepdims=True) * (1.0 / groups)
     lane = lax.broadcasted_iota(jnp.int32, (1, LANES), 1)
-    both = jnp.where(lane < LANES // 2, image_sq, grad_sq)
+    both = jnp.where(lane < LANES // 4, image_sq, grad_sq)
     out_ref[...] = jnp.broadcast_to(both[None], out_ref.shape)
+    me, group = lax.axis_index("param"), lax.axis_index("sensor")
+    points, pad = gradient.shape
+    part = pad // groups
+
+    def send(target, edge):
+        tile = jnp.zeros((ROWS, LANES), F32)
+        for t in range(pad // LANES):
+            tile += jnp.where(group // 2 == t, edge[:, t * LANES : (t + 1) * LANES], 0.0)
+        tile = jnp.where(group % 2 == 1, tile, pltpu.roll(tile, part, 1))
+        rows = jnp.where(lane < part, both, tile)
+        for i in range(groups):
+            out_ref[target * groups + i] = rows[i : i + 1]
+
+    @pl.when(me > 0)
+    def _():
+        send(me - 1, gradient[:ROWS])
+
+    @pl.when(me < params - 1)
+    def _():
+        send(me + 1, gradient[points - ROWS :])
 
 
 def shape(*dims):
@@ -302,12 +374,11 @@
     params = lax.axis_size("param")
     groups = lax.axis_size("sensor")
     assert params == sensors // ROWS * tiles and dips == ROWS
-    assert cols * (steps % LANES) <= LANES
+    assert cols * (steps % LANES) <= LANES and groups == dips and groups * LANES == 2 * pad
     high, low = (jnp.asarray(part) for part in dft_table(steps, freqs, pad))
     tiled = shape(params, ROWS, LANES)
     field = shape(points, pad)
     work = [(cols, dips, 2 * pad), (sensors, 2 * pad), kernel_spec.shape, pltpu.SemaphoreType.DMA((cols,))]
-    table = pltpu.VMEM(high.shape, BF16)
     swap = functools.partial(lax.all_to_all, split_axis=0, concat_axis=0)
     stay = functools.partial(pltpu.with_memory_space_constraint, memory_space=pltpu.HBM)
     spec = stay(kernel_spec)
@@ -316,39 +387,44 @@
     edge = shape(dips, pad)
     map_work = work[:2]
 
+    count = cols * (steps // LANES) + 1
+    back = (shape(groups, count, ROWS, LANES), shape(sensors, steps))
+    table = jax.ShapeDtypeStruct(high.shape, BF16)
     for iteration in range(ITERS):
         if iteration == 0:
-            parts, sources, inner, outer = call(
+            parts, sources, inner, outer, high, low = call(
                 functools.partial(first_kernel, steps),
-                (tiled, field, edge, edge),
-                work + [table, table, pltpu.VMEM(initial.shape, F32), pltpu.SemaphoreType.DMA((3,))],
+                (tiled, field, edge, edge, table, table),
+                work + [pltpu.VMEM(initial.shape, F32), pltpu.SemaphoreType.DMA((3,))],
                 outside=(0, 1, 2, 3),
                 inputs=4,
             )(stay(initial), spec, stay(high), stay(low))
-        else:
-            sources, inner, outer = call(step_kernel, (field, edge, edge))(sources, gradient, sums)
-            parts = call(functools.partial(map_kernel, steps), tiled, map_work)(
-                sources, kernel_spec, high, low
-            )
-        inner, outer = lax.ppermute(inner, "param", pairs), lax.ppermute(outer, "param", others)
-        if iteration == 0:
+            inner, outer = lax.ppermute(inner, "param", pairs), lax.ppermute(outer, "param", others)
             parts, inner, outer = lax.optimization_barrier((swap(parts, "param"), inner, outer))
         else:
-            parts, inner, outer = lax.optimization_barrier((parts, inner, outer))
+            parts, sources, inner, outer = call(
+                functools.partial(step_kernel, steps, params, groups), (tiled, field, edge, edge), map_work
+            )(sources, gradient, sums, inner, outer, held, high, low)
             parts = swap(parts, "param")
-        misfit = call(misfit_kernel, tiled, [(ROWS, pad)])(parts, observed)
-        count = cols * (steps // LANES) + 1
-        partial, residual = call(
-            functools.partial(adjoint_kernel, steps),
-            (shape(groups, count, ROWS, LANES), shape(sensors, steps)),
-            map_work,
-        )(swap(misfit, "param"), kernel_spec, high, low)
+        misfit = swap(call(misfit_kernel, tiled, [(ROWS, pad)])(parts, observed), "param")
+        if iteration == 0:
+            partial, residual, held = call(
+                functools.partial(first_adjoint_kernel, steps),
+                back + (shape(*kernel_spec.shape),),
+                map_work + work[3:],
+                outside=(3,),
+                inputs=6,
+            )(misfit, inner, outer, spec, high, low)
+        else:
+            partial, residual = call(functools.partial(adjoint_kernel, steps), back, map_work)(
+                misfit, inner, outer, held, high, low
+            )
         image, gradient = call(functools.partial(gradient_kernel, steps), (tiled, field), map_work)(
-            swap(partial, "sensor"), sources, inner, outer, kernel_spec, high, low
+            swap(partial, "sensor"), sources, held, high, low
         )
-        squares = call(functools.partial(squares_kernel, groups), shape(params * groups, 1, LANES))(
-            swap(image, "param"), gradient
-        )
+        squares = call(
+            functools.partial(squares_kernel, params, groups), shape(params * groups, 1, LANES)
+        )(swap(image, "param"), gradient)
         sums = swap(squares, ("param", "sensor"))
     sources = call(last_kernel, shape(cols, dips, steps))(sources, gradient, sums)
     return (sources, residual)

time: 180 us -> 174 us (0.967)
  starting transfers between devices: 18.1 us -> 14.9 us
  local copies, waits for them, and re-layouts: 2.81 us -> 0.01 us
  Pallas kernels: 19.5 us -> 21.7 us
  blocking collectives: 132 us -> 130 us
    unnamed x12 -> x2, local copies, waits for them, and re-layouts: 2.81 us -> 0.01 us
    ppermute x2 -> x1, starting transfers between devices: 5.61 us -> 3.41 us  [body(): lax.ppermute(outer, 'param', others)]
    pallas_call x9 -> x8, Pallas kernels: 14.1 us -> 16.2 us  [the longest x1 5.91 us: body(): call(functools.partial(first_kernel, steps), (tiled, field, edge, edge, t...]
  transfers between devices with their start and end apart: 5 -> 3, of which waited for: 3 -> 2; matrix products, arithmetic and copies ran while one was open for 0% -> 0% of each run, Pallas kernels for 1% -> 0%
where the time goes in v3:
time: 174 us; the launch traced here: 173 us
  blocking collectives  130 us (75%)
  Pallas kernels  21.7 us (12%)
  starting transfers between devices  14.9 us (9%)
  waiting for transfers between devices  5.48 us (3%)
    all_to_all x2, blocking collectives, body(): sums = swap(squares, ('param', 'sensor'))  36.1 us
    all_to_all x2, blocking collectives, body(): swap(partial, 'sensor')  27.9 us
    all_to_all x2, blocking collectives, body(): swap(call(misfit_kernel, tiled, [(ROWS, pad)])(parts, observed), 'param')  27 us
    all_to_all x2, blocking collectives, body(): swap(image, 'param')  26.5 us
    all_to_all x1, blocking collectives, body(): parts = swap(parts, 'param')  13 us
    all_to_all x1, starting transfers between devices, body(): swap(parts, 'param')  11.1 us
    pallas_call x1, Pallas kernels, body(): call(functools.partial(first_kernel, steps), (tiled, field, edge, edge, t...  5.91 us
    pallas_call x1, Pallas kernels, body(): call(functools.partial(first_adjoint_kernel, steps), back + (shape(*kerne...  4.33 us
  transfers between devices with their start and end apart: 3, of which 2 were waited for; matrix products, arithmetic and copies ran while one was open for 0% of the time, Pallas kernels for 0%

profile of v3, /device:TPU:1, one launch (start us, length us, event | category | flops | bytes accessed | tf_op | source)
XLA Modules:
  0.0 173.2 jit_solution(12390231602342642747)
XLA Ops:
  0.6 5.9 %shard_map.68 = (f32[32,8,128]{2,1,0:T(8,128)}, f32[24,512]{1,0:T(8,128)S(1)}, f32[8,512]{1,0:T(8,128)S(1)}, f32[8,512]{1,0:T(8,128)S(1)}, bf16[512,1024]{1,0:T(8,128)(2,1)S(1)}, /*index=5*/bf16[512,1024]{1,0:T(8,128)(2,1)S(1)}) custom-call(f32[3,8,420]{2,1,0:T(8,128)} %s_any.1, f32[2,3,8,64,421]{4,3,2,1,0:T(8,128)} %k_any.3, ...), custom_call_target="tpu_custom_call" | custom-call | tf_op jit(solution)/shard_map/pallas_call | solution.py:395
  6.6 11.1 %all-to-all-start = ((f32[32,8,128]{2,1,0:T(8,128)}), f32[32,8,128]{2,1,0:T(8,128)S(1)}, u32[]{:S(2)}, u32[]{:S(2)}) async-start(f32[32,8,128]{2,1,0:T(8,128)} %get-tuple-element.24), calls=%async_computation | async-start | bytes 262144 | tf_op jit(solution)/shard_map/all_to_all | solution.py:403
  17.7 0.3 collective-permute-start
  18.0 3.4 %collective-permute-start.1 = (f32[8,512]{1,0:T(8,128)S(1)}, f32[8,512]{1,0:T(8,128)S(1)}, u32[]{:S(2)}, u32[]{:S(2)}) collective-permute-start(f32[8,512]{1,0:T(8,128)S(1)} %get-tuple-element.26), channel_id=1, source_target_pairs={{8,16},{16,8},{24,32},{32,24},{40,48},{48,40},{56,64},{64,56},{72,... | collective-permute-start | bytes 49160 | tf_op jit(solution)/shard_map/ppermute | solution.py:402
  21.4 0.0 collective-permute-done.inner_ref
  21.4 2.0 %collective-permute-done.1.outer_ref = f32[8,512]{1,0:T(8,128)S(1)} collective-permute-done((f32[8,512]{1,0:T(8,128)S(1)}, f32[8,512]{1,0:T(8,128)S(1)}, u32[]{:S(2)}, u32[]{:S(2)}) %collective-permute-start.1) | collective-permute-done | bytes 16416 | tf_op jit(solution)/shard_map/ppermute | solution.py:402
  23.5 3.4 %all-to-all-done.parts_ref = f32[32,8,128]{2,1,0:T(8,128)S(1)} async-done(((f32[32,8,128]{2,1,0:T(8,128)}), f32[32,8,128]{2,1,0:T(8,128)S(1)}, u32[]{:S(2)}, u32[]{:S(2)}) %all-to-all-start) | async-done | bytes 131104 | tf_op jit(solution)/shard_map/all_to_all | solution.py:403
  27.0 14.5 %all_to_all.50.r_ref = f32[32,8,128]{2,1,0:T(8,128)S(1)} all-to-all(f32[32,8,128]{2,1,0:T(8,128)S(1)} %shard_map.69), channel_id=1, replica_groups=mesh['param'=32,'sensor'=8] {'param'}, dimensions={0} | all-to-all | bytes 262144 | tf_op jit(solution)/shard_map/all_to_all | solution.py:409
  41.5 4.3 %shard_map.70 = (f32[8,10,8,128]{3,2,1,0:T(8,128)S(1)}, f32[64,420]{1,0:T(8,128)}, f32[2,3,8,64,421]{4,3,2,1,0:T(8,128)S(1)}) custom-call(f32[32,8,128]{2,1,0:T(8,128)S(1)} %all_to_all.50.r_ref, f32[8,512]{1,0:T(8,128)S(1)} %collective-permute-done.inner_ref, f32[8,512]{1,0:T(8,128)S(1)} %collective-permute-done.1.outer_ref, f32[2,3,8,64,421]{4,3,2,1,0:T(8,128)} %k_any.3, ...), custom_call_target="tpu_custom_call" | custom-call | tf_op jit(solution)/shard_map/pallas_call | solution.py:411
  45.9 15.5 %all_to_all.51.parts_ref = f32[8,10,8,128]{3,2,1,0:T(8,128)S(1)} all-to-all(f32[8,10,8,128]{3,2,1,0:T(8,128)S(1)} %get-tuple-element.32), channel_id=1, replica_groups=mesh['param'=32,'sensor'=8] {'sensor'}, dimensions={0} | all-to-all | bytes 655360 | tf_op jit(solution)/shard_map/all_to_all | solution.py:423
  61.4 2.1 %shard_map.71 = (f32[32,8,128]{2,1,0:T(8,128)S(1)}, f32[24,512]{1,0:T(8,128)S(1)}) custom-call(f32[8,10,8,128]{3,2,1,0:T(8,128)S(1)} %all_to_all.51.parts_ref, f32[24,512]{1,0:T(8,128)S(1)} %get-tuple-element.23.s_ref, f32[2,3,8,64,421]{4,3,2,1,0:T(8,128)S(1)} %get-tuple-element.33.k_ref, bf16[512,1024]{1,0:T(8,128)(2,1)S(1)} %get-tuple-element.30.high_ref, ...), custom_call_target="tpu_custom_call" | custom-call | tf_op jit(solution)/shard_map/pallas_call | solution.py:422
  63.5 13.2 %all_to_all.52.parts_ref = f32[32,8,128]{2,1,0:T(8,128)S(1)} all-to-all(f32[32,8,128]{2,1,0:T(8,128)S(1)} %get-tuple-element.35), channel_id=1, replica_groups=mesh['param'=32,'sensor'=8] {'param'}, dimensions={0} | all-to-all | bytes 262144 | tf_op jit(solution)/shard_map/all_to_all | solution.py:427
  76.8 0.4 shard_map.72
  77.1 18.0 %all_to_all.53.sums_ref = f32[256,1,128]{2,1,0:T(1,128)S(1)} all-to-all(f32[256,1,128]{2,1,0:T(1,128)S(1)} %shard_map.72), channel_id=1, replica_groups=mesh['param'=32,'sensor'=8] {'param','sensor'}, dimensions={0} | all-to-all | bytes 262144 | tf_op jit(solution)/shard_map/all_to_all | solution.py:428
  95.2 2.6 %shard_map.73 = (f32[32,8,128]{2,1,0:T(8,128)S(1)}, f32[24,512]{1,0:T(8,128)S(1)}, f32[8,512]{1,0:T(8,128)S(1)}, f32[8,512]{1,0:T(8,128)S(1)}) custom-call(f32[24,512]{1,0:T(8,128)S(1)} %get-tuple-element.23.s_ref, f32[24,512]{1,0:T(8,128)S(1)} %get-tuple-element.34.g_ref, f32[256,1,128]{2,1,0:T(1,128)S(1)} %all_to_all.53.sums_ref, ...), custom_call_target="tpu_custom_call" | custom-call | tf_op jit(solution)/shard_map/pallas_call | solution.py:405
  97.8 13.0 %all_to_all.54.parts_ref = f32[32,8,128]{2,1,0:T(8,128)S(1)} all-to-all(f32[32,8,128]{2,1,0:T(8,128)S(1)} %get-tuple-element.37), channel_id=1, replica_groups=mesh['param'=32,'sensor'=8] {'param'}, dimensions={0} | all-to-all | bytes 262144 | tf_op jit(solution)/shard_map/all_to_all | solution.py:408
  110.9 12.4 %all_to_all.55.r_ref = f32[32,8,128]{2,1,0:T(8,128)S(1)} all-to-all(f32[32,8,128]{2,1,0:T(8,128)S(1)} %shard_map.74), channel_id=1, replica_groups=mesh['param'=32,'sensor'=8] {'param'}, dimensions={0} | all-to-all | bytes 262144 | tf_op jit(solution)/shard_map/all_to_all | solution.py:409
  123.4 2.5 %shard_map.75 = (f32[8,10,8,128]{3,2,1,0:T(8,128)S(1)}, f32[64,420]{1,0:T(8,128)}) custom-call(f32[32,8,128]{2,1,0:T(8,128)S(1)} %all_to_all.55.r_ref, f32[8,512]{1,0:T(8,128)S(1)} %get-tuple-element.38.inner_ref, f32[8,512]{1,0:T(8,128)S(1)} %get-tuple-element.39.outer_ref, f32[2,3,8,64,421]{4,3,2,1,0:T(8,128)S(1)} %get-tuple-element.33.k_ref, ...), custom_call_target="tpu_custom_call" | custom-call | tf_op jit(solution)/shard_map/pallas_call | solution.py:419
  125.9 12.4 %all_to_all.56.parts_ref = f32[8,10,8,128]{3,2,1,0:T(8,128)S(1)} all-to-all(f32[8,10,8,128]{3,2,1,0:T(8,128)S(1)} %get-tuple-element.40), channel_id=1, replica_groups=mesh['param'=32,'sensor'=8] {'sensor'}, dimensions={0} | all-to-all | bytes 655360 | tf_op jit(solution)/shard_map/all_to_all | solution.py:423
  138.2 2.1 %shard_map.76 = (f32[32,8,128]{2,1,0:T(8,128)S(1)}, f32[24,512]{1,0:T(8,128)S(1)}) custom-call(f32[8,10,8,128]{3,2,1,0:T(8,128)S(1)} %all_to_all.56.parts_ref, f32[24,512]{1,0:T(8,128)S(1)} %get-tuple-element.36.s_ref, f32[2,3,8,64,421]{4,3,2,1,0:T(8,128)S(1)} %get-tuple-element.33.k_ref, bf16[512,1024]{1,0:T(8,128)(2,1)S(1)} %get-tuple-element.30.high_ref, ...), custom_call_target="tpu_custom_call" | custom-call | tf_op jit(solution)/shard_map/pallas_call | solution.py:422
  140.4 13.2 %all_to_all.57.parts_ref = f32[32,8,128]{2,1,0:T(8,128)S(1)} all-to-all(f32[32,8,128]{2,1,0:T(8,128)S(1)} %get-tuple-element.42), channel_id=1, replica_groups=mesh['param'=32,'sensor'=8] {'param'}, dimensions={0} | all-to-all | bytes 262144 | tf_op jit(solution)/shard_map/all_to_all | solution.py:427
  153.6 0.4 shard_map.77
  154.0 18.0 %all_to_all.58.sums_ref = f32[256,1,128]{2,1,0:T(1,128)S(1)} all-to-all(f32[256,1,128]{2,1,0:T(1,128)S(1)} %shard_map.77), channel_id=1, replica_groups=mesh['param'=32,'sensor'=8] {'param','sensor'}, dimensions={0} | all-to-all | bytes 262144 | tf_op jit(solution)/shard_map/all_to_all | solution.py:428
  172.1 1.1 shard_map.78
  (4 shorter events, 0.1 us)
Async XLA Ops:
  0.6 26.3 %copy-start = (f32[64,420]{1,0:T(8,128)S(1)}, f32[64,420]{1,0:T(8,128)}, u32[]{:S(2)}) copy-start(f32[64,420]{1,0:T(8,128)} %observed_ref.3) | copy-start | bytes 322564
  6.6 20.4 %all-to-all-start = ((f32[32,8,128]{2,1,0:T(8,128)}), f32[32,8,128]{2,1,0:T(8,128)S(1)}, u32[]{:S(2)}, u32[]{:S(2)}) async-start(f32[32,8,128]{2,1,0:T(8,128)} %get-tuple-element.24), calls=%async_computation | async-start | bytes 262144 | tf_op jit(solution)/shard_map/all_to_all | solution.py:403
  17.7 3.7 %collective-permute-start = (f32[8,512]{1,0:T(8,128)S(1)}, f32[8,512]{1,0:T(8,128)S(1)}, u32[]{:S(2)}, u32[]{:S(2)}) collective-permute-start(f32[8,512]{1,0:T(8,128)S(1)} %get-tuple-element.25), channel_id=1, source_target_pairs={{0,8},{8,0},{16,24},{24,16},{32,40},{40,32},{48,56},{56,48},{64,72... | collective-permute-start | bytes 49160 | tf_op jit(solution)/shard_map/ppermute | solution.py:402
  18.0 5.5 %collective-permute-start.1 = (f32[8,512]{1,0:T(8,128)S(1)}, f32[8,512]{1,0:T(8,128)S(1)}, u32[]{:S(2)}, u32[]{:S(2)}) collective-permute-start(f32[8,512]{1,0:T(8,128)S(1)} %get-tuple-element.26), channel_id=1, source_target_pairs={{8,16},{16,8},{24,32},{32,24},{40,48},{48,40},{56,64},{64,56},{72,... | collective-permute-start | bytes 49160 | tf_op jit(solution)/shard_map/ppermute | solution.py:402

commit v4 on v3

--- a/solution.py
+++ b/solution.py
@@ -68,7 +68,7 @@
     pad = field.shape[1]
     xs_ref[...] = product(field, high_ref, low_ref, slice(0, 2 * pad)).reshape(cols, dips, 2 * pad)
     ys_ref[...] = jnp.zeros_like(ys_ref)
-    height = min(32, sensors)
+    height = min(8, sensors)
 
     def column(c, carry):
         if sems is not None:
@@ -76,20 +76,17 @@
         for start, width in lane_blocks(freqs):
             for top in range(0, sensors, height):
                 rows = slice(top, top + height)
-                rr = ys_ref[rows, start : start + width]
-                ri = ys_ref[rows, pad + start : pad + start + width]
-                ii = ir = jnp.zeros((height, width), F32)
+                real = ys_ref[rows, start : start + width]
+                imag = ys_ref[rows, pad + start : pad + start + width]
                 for d in range(dips):
                     kr = k_ref[0, c, d, rows, start : start + width]
                     ki = k_ref[1, c, d, rows, start : start + width]
                     xr = xs_ref[c, d : d + 1, start : start + width]
                     xi = xs_ref[c, d : d + 1, pad + start : pad + start + width]
-                    rr = rr + kr * xr
-                    ii = ii + ki * xi
-                    ri = ri + kr * xi
-                    ir = ir + ki * xr
-                ys_ref[rows, start : start + width] = rr - ii
-                ys_ref[rows, pad + start : pad + start + width] = ri + ir
+                    real = real + (kr * xr - ki * xi)
+                    imag = imag + (kr * xi + ki * xr)
+                ys_ref[rows, start : start + width] = real
+                ys_ref[rows, pad + start : pad + start + width] = imag
         return carry
 
     lax.fori_loop(0, cols, column, 0)
@@ -147,7 +144,7 @@
 
 
 def step_size(sums_ref):
-    sums = jnp.sum(sums_ref[...], axis=0)
+    sums = jnp.sum(jnp.sum(sums_ref[...], axis=0), axis=0, keepdims=True)
     image_sq = sums[:, :1]
     grad_sq = sums[:, LANES // 4 : LANES // 4 + 1]
     return grad_sq / (image_sq + 8.0 * LAMBDA_REG * grad_sq + TINY_TERM)
@@ -157,20 +154,19 @@
     return jnp.maximum(field - alpha * gradient, 0.0)
 
 
-def gathered_row(sums_ref, neighbour, exists, groups):
+def gathered_row(sums_ref, neighbour, exists):
     lane = lax.broadcasted_iota(jnp.int32, (1, LANES), 1)
-    start = jnp.where(exists, neighbour, 0) * groups
-    tiles = []
-    for i in range(0, groups, 2):
-        low, high = sums_ref[start + i], sums_ref[start + i + 1]
-        tiles.append(jnp.where(lane < LANES // 2, pltpu.roll(low, LANES // 2, 1), high))
+    came = sums_ref[jnp.where(exists, neighbour, 0)]
+    turned = pltpu.roll(came, LANES // 2, 1)
+    tiles = [
+        jnp.where(lane < LANES // 2, turned[i : i + 1], came[i + 1 : i + 2]) for i in range(0, came.shape[0], 2)
+    ]
     return jnp.where(exists, jnp.concatenate(tiles, axis=1), 0.0)
 
 
 def step_kernel(
     steps,
     params,
-    groups,
     s_ref,
     g_ref,
     sums_ref,
@@ -191,8 +187,8 @@
     alpha = step_size(sums_ref)
     new = stepped(s_ref[...], g_ref[...], alpha)
     new_ref[...] = new
-    below = gathered_row(sums_ref, me - 1, me > 0, groups)
-    above = gathered_row(sums_ref, me + 1, me < params - 1, groups)
+    below = gathered_row(sums_ref, me - 1, me > 0)
+    above = gathered_row(sums_ref, me + 1, me < params - 1)
     new_inner_ref[...] = stepped(inner_ref[...], jnp.where(even, above, below), alpha)
     new_outer_ref[...] = stepped(outer_ref[...], jnp.where(even, below, above), alpha)
     forward_map(new, None, high_ref, low_ref, out_ref, xs_ref, ys_ref, k_ref, None, steps)
@@ -337,9 +333,7 @@
         for t in range(pad // LANES):
             tile += jnp.where(group // 2 == t, edge[:, t * LANES : (t + 1) * LANES], 0.0)
         tile = jnp.where(group % 2 == 1, tile, pltpu.roll(tile, part, 1))
-        rows = jnp.where(lane < part, both, tile)
-        for i in range(groups):
-            out_ref[target * groups + i] = rows[i : i + 1]
+        out_ref[target] = jnp.where(lane < part, both, tile)
 
     @pl.when(me > 0)
     def _():
@@ -403,7 +397,7 @@
             parts, inner, outer = lax.optimization_barrier((swap(parts, "param"), inner, outer))
         else:
             parts, sources, inner, outer = call(
-                functools.partial(step_kernel, steps, params, groups), (tiled, field, edge, edge), map_work
+                functools.partial(step_kernel, steps, params), (tiled, field, edge, edge), map_work
             )(sources, gradient, sums, inner, outer, held, high, low)
             parts = swap(parts, "param")
         misfit = swap(call(misfit_kernel, tiled, [(ROWS, pad)])(parts, observed), "param")
@@ -422,10 +416,11 @@
         image, gradient = call(functools.partial(gradient_kernel, steps), (tiled, field), map_work)(
             swap(partial, "sensor"), sources, held, high, low
         )
-        squares = call(
-            functools.partial(squares_kernel, params, groups), shape(params * groups, 1, LANES)
-        )(swap(image, "param"), gradient)
-        sums = swap(squares, ("param", "sensor"))
+        squares = call(functools.partial(squares_kernel, params, groups), shape(params, groups, LANES))(
+            swap(image, "param"), gradient
+        )
+        sums = swap(squares.reshape(params * groups, 1, LANES), ("param", "sensor"))
+        sums = sums.reshape(params, groups, LANES)
     sources = call(last_kernel, shape(cols, dips, steps))(sources, gradient, sums)
     return (sources, residual)
 

time: 174 us -> 172 us (0.989)
  no operation moved by 1% of the time
where the time goes in v4:
time: 172 us; the launch traced here: 171 us
  blocking collectives  130 us (76%)
  Pallas kernels  20 us (12%)
  starting transfers between devices  14.9 us (9%)
  waiting for transfers between devices  5.48 us (3%)
    all_to_all x2, blocking collectives, body(): sums = swap(squares.reshape(params * groups, 1, LANES), ('param', 'sensor'))  36.1 us
    all_to_all x2, blocking collectives, body(): swap(partial, 'sensor')  27.9 us
    all_to_all x2, blocking collectives, body(): swap(call(misfit_kernel, tiled, [(ROWS, pad)])(parts, observed), 'param')  27 us
    all_to_all x2, blocking collectives, body(): swap(image, 'param')  26.5 us
    all_to_all x1, blocking collectives, body(): parts = swap(parts, 'param')  13 us
    all_to_all x1, starting transfers between devices, body(): swap(parts, 'param')  11.1 us
    pallas_call x1, Pallas kernels, body(): call(functools.partial(first_kernel, steps), (tiled, field, edge, edge, t...  5.48 us
    pallas_call x1, Pallas kernels, body(): call(functools.partial(first_adjoint_kernel, steps), back + (shape(*kerne...  4.33 us
  transfers between devices with their start and end apart: 3, of which 2 were waited for; matrix products, arithmetic and copies ran while one was open for 0% of the time, Pallas kernels for 0%

profile of v4, /device:TPU:1, one launch (start us, length us, event | category | flops | bytes accessed | tf_op | source)
XLA Modules:
  0.0 171.5 jit_solution(1464048984478143357)
XLA Ops:
  0.6 5.5 %shard_map.68 = (f32[32,8,128]{2,1,0:T(8,128)}, f32[24,512]{1,0:T(8,128)S(1)}, f32[8,512]{1,0:T(8,128)S(1)}, f32[8,512]{1,0:T(8,128)S(1)}, bf16[512,1024]{1,0:T(8,128)(2,1)S(1)}, /*index=5*/bf16[512,1024]{1,0:T(8,128)(2,1)S(1)}) custom-call(f32[3,8,420]{2,1,0:T(8,128)} %s_any.1, f32[2,3,8,64,421]{4,3,2,1,0:T(8,128)} %k_any.3, ...), custom_call_target="tpu_custom_call" | custom-call | tf_op jit(solution)/shard_map/pallas_call | solution.py:389
  6.1 11.1 %all-to-all-start = ((f32[32,8,128]{2,1,0:T(8,128)}), f32[32,8,128]{2,1,0:T(8,128)S(1)}, u32[]{:S(2)}, u32[]{:S(2)}) async-start(f32[32,8,128]{2,1,0:T(8,128)} %get-tuple-element.24), calls=%async_computation | async-start | bytes 262144 | tf_op jit(solution)/shard_map/all_to_all | solution.py:397
  17.3 0.3 collective-permute-start
  17.6 3.4 %collective-permute-start.1 = (f32[8,512]{1,0:T(8,128)S(1)}, f32[8,512]{1,0:T(8,128)S(1)}, u32[]{:S(2)}, u32[]{:S(2)}) collective-permute-start(f32[8,512]{1,0:T(8,128)S(1)} %get-tuple-element.26), channel_id=1, source_target_pairs={{8,16},{16,8},{24,32},{32,24},{40,48},{48,40},{56,64},{64,56},{72,... | collective-permute-start | bytes 49160 | tf_op jit(solution)/shard_map/ppermute | solution.py:396
  21.0 0.0 collective-permute-done.inner_ref
  21.0 2.0 %collective-permute-done.1.outer_ref = f32[8,512]{1,0:T(8,128)S(1)} collective-permute-done((f32[8,512]{1,0:T(8,128)S(1)}, f32[8,512]{1,0:T(8,128)S(1)}, u32[]{:S(2)}, u32[]{:S(2)}) %collective-permute-start.1) | collective-permute-done | bytes 16416 | tf_op jit(solution)/shard_map/ppermute | solution.py:396
  23.1 3.4 %all-to-all-done.parts_ref = f32[32,8,128]{2,1,0:T(8,128)S(1)} async-done(((f32[32,8,128]{2,1,0:T(8,128)}), f32[32,8,128]{2,1,0:T(8,128)S(1)}, u32[]{:S(2)}, u32[]{:S(2)}) %all-to-all-start) | async-done | bytes 131104 | tf_op jit(solution)/shard_map/all_to_all | solution.py:397
  26.5 14.5 %all_to_all.50.r_ref = f32[32,8,128]{2,1,0:T(8,128)S(1)} all-to-all(f32[32,8,128]{2,1,0:T(8,128)S(1)} %shard_map.69), channel_id=1, replica_groups=mesh['param'=32,'sensor'=8] {'param'}, dimensions={0} | all-to-all | bytes 262144 | tf_op jit(solution)/shard_map/all_to_all | solution.py:403
  41.1 4.3 %shard_map.70 = (f32[8,10,8,128]{3,2,1,0:T(8,128)S(1)}, f32[64,420]{1,0:T(8,128)}, f32[2,3,8,64,421]{4,3,2,1,0:T(8,128)S(1)}) custom-call(f32[32,8,128]{2,1,0:T(8,128)S(1)} %all_to_all.50.r_ref, f32[8,512]{1,0:T(8,128)S(1)} %collective-permute-done.inner_ref, f32[8,512]{1,0:T(8,128)S(1)} %collective-permute-done.1.outer_ref, f32[2,3,8,64,421]{4,3,2,1,0:T(8,128)} %k_any.3, ...), custom_call_target="tpu_custom_call" | custom-call | tf_op jit(solution)/shard_map/pallas_call | solution.py:405
  45.4 15.5 %all_to_all.51.parts_ref = f32[8,10,8,128]{3,2,1,0:T(8,128)S(1)} all-to-all(f32[8,10,8,128]{3,2,1,0:T(8,128)S(1)} %get-tuple-element.32), channel_id=1, replica_groups=mesh['param'=32,'sensor'=8] {'sensor'}, dimensions={0} | all-to-all | bytes 655360 | tf_op jit(solution)/shard_map/all_to_all | solution.py:417
  61.0 1.9 %shard_map.71 = (f32[32,8,128]{2,1,0:T(8,128)S(1)}, f32[24,512]{1,0:T(8,128)S(1)}) custom-call(f32[8,10,8,128]{3,2,1,0:T(8,128)S(1)} %all_to_all.51.parts_ref, f32[24,512]{1,0:T(8,128)S(1)} %get-tuple-element.23.s_ref, f32[2,3,8,64,421]{4,3,2,1,0:T(8,128)S(1)} %get-tuple-element.33.k_ref, bf16[512,1024]{1,0:T(8,128)(2,1)S(1)} %get-tuple-element.30.high_ref, ...), custom_call_target="tpu_custom_call" | custom-call | tf_op jit(solution)/shard_map/pallas_call | solution.py:416
  62.9 13.2 %all_to_all.52.parts_ref = f32[32,8,128]{2,1,0:T(8,128)S(1)} all-to-all(f32[32,8,128]{2,1,0:T(8,128)S(1)} %get-tuple-element.35), channel_id=1, replica_groups=mesh['param'=32,'sensor'=8] {'param'}, dimensions={0} | all-to-all | bytes 262144 | tf_op jit(solution)/shard_map/all_to_all | solution.py:420
  76.1 0.3 shard_map.72
  76.4 18.0 %all_to_all.53 = f32[256,1,128]{2,1,0:T(1,128)S(1)} all-to-all(f32[256,1,128]{2,1,0:T(1,128)S(1)} %bitcast.10), channel_id=1, replica_groups=mesh['param'=32,'sensor'=8] {'param','sensor'}, dimensions={0} | all-to-all | bytes 262144 | tf_op jit(solution)/shard_map/all_to_all | solution.py:422
  94.5 2.2 %shard_map.73 = (f32[32,8,128]{2,1,0:T(8,128)S(1)}, f32[24,512]{1,0:T(8,128)S(1)}, f32[8,512]{1,0:T(8,128)S(1)}, f32[8,512]{1,0:T(8,128)S(1)}) custom-call(f32[24,512]{1,0:T(8,128)S(1)} %get-tuple-element.23.s_ref, f32[24,512]{1,0:T(8,128)S(1)} %get-tuple-element.34.g_ref, f32[32,8,128]{2,1,0:T(8,128)S(1)} %bitcast.8, ...), custom_call_target="tpu_custom_call" | custom-call | tf_op jit(solution)/shard_map/pallas_call | solution.py:399
  96.6 13.0 %all_to_all.54.parts_ref = f32[32,8,128]{2,1,0:T(8,128)S(1)} all-to-all(f32[32,8,128]{2,1,0:T(8,128)S(1)} %get-tuple-element.37), channel_id=1, replica_groups=mesh['param'=32,'sensor'=8] {'param'}, dimensions={0} | all-to-all | bytes 262144 | tf_op jit(solution)/shard_map/all_to_all | solution.py:402
  109.7 12.4 %all_to_all.55.r_ref = f32[32,8,128]{2,1,0:T(8,128)S(1)} all-to-all(f32[32,8,128]{2,1,0:T(8,128)S(1)} %shard_map.74), channel_id=1, replica_groups=mesh['param'=32,'sensor'=8] {'param'}, dimensions={0} | all-to-all | bytes 262144 | tf_op jit(solution)/shard_map/all_to_all | solution.py:403
  122.2 2.5 %shard_map.75 = (f32[8,10,8,128]{3,2,1,0:T(8,128)S(1)}, f32[64,420]{1,0:T(8,128)}) custom-call(f32[32,8,128]{2,1,0:T(8,128)S(1)} %all_to_all.55.r_ref, f32[8,512]{1,0:T(8,128)S(1)} %get-tuple-element.38.inner_ref, f32[8,512]{1,0:T(8,128)S(1)} %get-tuple-element.39.outer_ref, f32[2,3,8,64,421]{4,3,2,1,0:T(8,128)S(1)} %get-tuple-element.33.k_ref, ...), custom_call_target="tpu_custom_call" | custom-call | tf_op jit(solution)/shard_map/pallas_call | solution.py:413
  124.7 12.4 %all_to_all.56.parts_ref = f32[8,10,8,128]{3,2,1,0:T(8,128)S(1)} all-to-all(f32[8,10,8,128]{3,2,1,0:T(8,128)S(1)} %get-tuple-element.40), channel_id=1, replica_groups=mesh['param'=32,'sensor'=8] {'sensor'}, dimensions={0} | all-to-all | bytes 655360 | tf_op jit(solution)/shard_map/all_to_all | solution.py:417
  137.1 1.9 %shard_map.76 = (f32[32,8,128]{2,1,0:T(8,128)S(1)}, f32[24,512]{1,0:T(8,128)S(1)}) custom-call(f32[8,10,8,128]{3,2,1,0:T(8,128)S(1)} %all_to_all.56.parts_ref, f32[24,512]{1,0:T(8,128)S(1)} %get-tuple-element.36.s_ref, f32[2,3,8,64,421]{4,3,2,1,0:T(8,128)S(1)} %get-tuple-element.33.k_ref, bf16[512,1024]{1,0:T(8,128)(2,1)S(1)} %get-tuple-element.30.high_ref, ...), custom_call_target="tpu_custom_call" | custom-call | tf_op jit(solution)/shard_map/pallas_call | solution.py:416
  139.0 13.2 %all_to_all.57.parts_ref = f32[32,8,128]{2,1,0:T(8,128)S(1)} all-to-all(f32[32,8,128]{2,1,0:T(8,128)S(1)} %get-tuple-element.42), channel_id=1, replica_groups=mesh['param'=32,'sensor'=8] {'param'}, dimensions={0} | all-to-all | bytes 262144 | tf_op jit(solution)/shard_map/all_to_all | solution.py:420
  152.2 0.3 shard_map.77
  152.5 18.0 %all_to_all.58 = f32[256,1,128]{2,1,0:T(1,128)S(1)} all-to-all(f32[256,1,128]{2,1,0:T(1,128)S(1)} %bitcast.11), channel_id=1, replica_groups=mesh['param'=32,'sensor'=8] {'param','sensor'}, dimensions={0} | all-to-all | bytes 262144 | tf_op jit(solution)/shard_map/all_to_all | solution.py:422
  170.6 0.9 shard_map.78
  (4 shorter events, 0.1 us)
Async XLA Ops:
  0.6 25.9 %copy-start = (f32[64,420]{1,0:T(8,128)S(1)}, f32[64,420]{1,0:T(8,128)}, u32[]{:S(2)}) copy-start(f32[64,420]{1,0:T(8,128)} %observed_ref.3) | copy-start | bytes 322564
  6.1 20.4 %all-to-all-start = ((f32[32,8,128]{2,1,0:T(8,128)}), f32[32,8,128]{2,1,0:T(8,128)S(1)}, u32[]{:S(2)}, u32[]{:S(2)}) async-start(f32[32,8,128]{2,1,0:T(8,128)} %get-tuple-element.24), calls=%async_computation | async-start | bytes 262144 | tf_op jit(solution)/shard_map/all_to_all | solution.py:397
  17.3 3.7 %collective-permute-start = (f32[8,512]{1,0:T(8,128)S(1)}, f32[8,512]{1,0:T(8,128)S(1)}, u32[]{:S(2)}, u32[]{:S(2)}) collective-permute-start(f32[8,512]{1,0:T(8,128)S(1)} %get-tuple-element.25), channel_id=1, source_target_pairs={{0,8},{8,0},{16,24},{24,16},{32,40},{40,32},{48,56},{56,48},{64,72... | collective-permute-start | bytes 49160 | tf_op jit(solution)/shard_map/ppermute | solution.py:396
  17.6 5.5 %collective-permute-start.1 = (f32[8,512]{1,0:T(8,128)S(1)}, f32[8,512]{1,0:T(8,128)S(1)}, u32[]{:S(2)}, u32[]{:S(2)}) collective-permute-start(f32[8,512]{1,0:T(8,128)S(1)} %get-tuple-element.26), channel_id=1, source_target_pairs={{8,16},{16,8},{24,32},{32,24},{40,48},{48,40},{56,64},{64,56},{72,... | collective-permute-start | bytes 49160 | tf_op jit(solution)/shard_map/ppermute | solution.py:396

commit v5 on v4

--- a/solution.py
+++ b/solution.py
@@ -8,6 +8,7 @@
 from jax.experimental import pallas as pl
 from jax.experimental.pallas import tpu as pltpu
 from jax.sharding import PartitionSpec as P
+
 
 ITERS = 2
 LAMBDA_REG = 0.5
@@ -116,9 +117,9 @@
     outer_ref,
     high_ref,
     low_ref,
+    k_ref,
     xs_ref,
     ys_ref,
-    k_ref,
     sems,
     s_ref,
     table_sems,
@@ -240,9 +241,8 @@
 
 
 def adjoint_kernel(
-    steps, r_ref, inner_ref, outer_ref, k_ref, high_ref, low_ref, out_ref, res_ref, xs_ref, ys_ref, k_any=None, sems=None
+    steps, r_ref, inner_ref, outer_ref, k_ref, high_ref, low_ref, out_ref, res_ref, xs_ref, ys_ref
 ):
-    start_columns(k_any, k_ref, sems)
     _, cols, dips, sensors, freqs = k_ref.shape
     pad = xs_ref.shape[2] // 2
     tiles = pad // LANES
@@ -256,8 +256,6 @@
     xs_ref[...] = jnp.zeros_like(xs_ref)
 
     def column(c, carry):
-        if sems is not None:
-            column_copy(c, k_any, k_ref, sems).wait()
         for start, width in lane_blocks(freqs):
             rr = [ys_ref[top : top + ROWS, start : start + width] for top in range(0, sensors, ROWS)]
             ri = [ys_ref[top : top + ROWS, pad + start : pad + start + width] for top in range(0, sensors, ROWS)]
@@ -286,14 +284,6 @@
     for j, tile in enumerate(packed(series, cols, steps)):
         for i in range(out_ref.shape[0]):
             out_ref[i, j] = tile
-
-
-def first_adjoint_kernel(
-    steps, r_ref, inner_ref, outer_ref, k_any, high_ref, low_ref, out_ref, res_ref, k_ref, xs_ref, ys_ref, sems
-):
-    adjoint_kernel(
-        steps, r_ref, inner_ref, outer_ref, k_ref, high_ref, low_ref, out_ref, res_ref, xs_ref, ys_ref, k_any, sems
-    )
 
 
 def gradient_kernel(
@@ -372,7 +362,7 @@
     high, low = (jnp.asarray(part) for part in dft_table(steps, freqs, pad))
     tiled = shape(params, ROWS, LANES)
     field = shape(points, pad)
-    work = [(cols, dips, 2 * pad), (sensors, 2 * pad), kernel_spec.shape, pltpu.SemaphoreType.DMA((cols,))]
+    work = [(cols, dips, 2 * pad), (sensors, 2 * pad), pltpu.SemaphoreType.DMA((cols,))]
     swap = functools.partial(lax.all_to_all, split_axis=0, concat_axis=0)
     stay = functools.partial(pltpu.with_memory_space_constraint, memory_space=pltpu.HBM)
     spec = stay(kernel_spec)
@@ -386,33 +376,28 @@
     table = jax.ShapeDtypeStruct(high.shape, BF16)
     for iteration in range(ITERS):
         if iteration == 0:
-            parts, sources, inner, outer, high, low = call(
+            parts, sources, inner, outer, high, low, held = call(
                 functools.partial(first_kernel, steps),
-                (tiled, field, edge, edge, table, table),
+                (tiled, field, edge, edge, table, table, shape(*kernel_spec.shape)),
                 work + [pltpu.VMEM(initial.shape, F32), pltpu.SemaphoreType.DMA((3,))],
                 outside=(0, 1, 2, 3),
                 inputs=4,
             )(stay(initial), spec, stay(high), stay(low))
-            inner, outer = lax.ppermute(inner, "param", pairs), lax.ppermute(outer, "param", others)
-            parts, inner, outer = lax.optimization_barrier((swap(parts, "param"), inner, outer))
+            inner = lax.ppermute(inner, "param", pairs)
+            outer = lax.ppermute(outer, "param", others)
+            parts = swap(parts, "param")
         else:
             parts, sources, inner, outer = call(
                 functools.partial(step_kernel, steps, params), (tiled, field, edge, edge), map_work
             )(sources, gradient, sums, inner, outer, held, high, low)
             parts = swap(parts, "param")
-        misfit = swap(call(misfit_kernel, tiled, [(ROWS, pad)])(parts, observed), "param")
+        misfit = call(misfit_kernel, tiled, [(ROWS, pad)])(parts, observed)
         if iteration == 0:
-            partial, residual, held = call(
-                functools.partial(first_adjoint_kernel, steps),
-                back + (shape(*kernel_spec.shape),),
-                map_work + work[3:],
-                outside=(3,),
-                inputs=6,
-            )(misfit, inner, outer, spec, high, low)
-        else:
-            partial, residual = call(functools.partial(adjoint_kernel, steps), back, map_work)(
-                misfit, inner, outer, held, high, low
-            )
+            misfit, inner, outer = lax.optimization_barrier((misfit, inner, outer))
+        misfit = swap(misfit, "param")
+        partial, residual = call(functools.partial(adjoint_kernel, steps), back, map_work)(
+            misfit, inner, outer, held, high, low
+        )
         image, gradient = call(functools.partial(gradient_kernel, steps), (tiled, field), map_work)(
             swap(partial, "sensor"), sources, held, high, low
         )

time: 172 us -> 176 us (1.023)
  local copies, waits for them, and re-layouts: 0.01 us -> 5.43 us
  Pallas kernels: 20 us -> 18.2 us
    unnamed x2 -> x8, local copies, waits for them, and re-layouts: 0.01 us -> 5.43 us
    pallas_call x3 -> x2, Pallas kernels: 4.43 us -> 0.09 us  [body(): misfit = call(misfit_kernel, tiled, [(ROWS, pad)])(parts, observed)]
    pallas_call x1 -> x2, Pallas kernels: 2.54 us -> 5.12 us  [body(): call(functools.partial(adjoint_kernel, steps), back, map_work)]
    all_to_all x1, waiting for transfers between devices: 3.43 us -> 5.49 us  [body(): parts = swap(parts, 'param')]
    ppermute x2, waiting for transfers between devices: 2.05 us -> 0.01 us  [the longest x1 0.01 us: body(): outer = lax.ppermute(outer, 'param', others)]
  transfers between devices with their start and end apart: 3 -> 3, of which waited for: 2 -> 1; matrix products, arithmetic and copies ran while one was open for 0% -> 0% of each run, Pallas kernels for 0% -> 0%
where the time goes in v5:
time: 176 us; the launch traced here: 175 us
  blocking collectives  130 us (74%)
  Pallas kernels  18.2 us (10%)
  starting transfers between devices  14.9 us (8%)
  waiting for transfers between devices  5.49 us (3%)
  local copies, waits for them, and re-layouts  5.43 us (3%)
    all_to_all x2, blocking collectives, body(): sums = swap(squares.reshape(params * groups, 1, LANES), ('param', 'sensor'))  36.1 us
    all_to_all x2, blocking collectives, body(): swap(partial, 'sensor')  27.9 us
    all_to_all x2, blocking collectives, body(): misfit = swap(misfit, 'param')  26.9 us
    all_to_all x2, blocking collectives, body(): swap(image, 'param')  26.5 us
    all_to_all x1, blocking collectives, body(): parts = swap(parts, 'param')  13 us
    all_to_all x1, starting transfers between devices, body(): parts = swap(parts, 'param')  11.1 us
    all_to_all x1, waiting for transfers between devices, body(): parts = swap(parts, 'param')  5.49 us
    pallas_call x1, Pallas kernels, body(): call(functools.partial(first_kernel, steps), (tiled, field, edge, edge, t...  5.48 us
  transfers between devices with their start and end apart: 3, of which 1 were waited for; matrix products, arithmetic and copies ran while one was open for 0% of the time, Pallas kernels for 0%

profile of v5, /device:TPU:1, one launch (start us, length us, event | category | flops | bytes accessed | tf_op | source)
XLA Modules:
  0.0 175.1 jit_solution(3490996051308629137)
XLA Ops:
  0.6 5.5 %shard_map.68 = (f32[32,8,128]{2,1,0:T(8,128)}, f32[24,512]{1,0:T(8,128)S(1)}, f32[8,512]{1,0:T(8,128)S(1)}, f32[8,512]{1,0:T(8,128)S(1)}, bf16[512,1024]{1,0:T(...) custom-call(f32[3,8,420]{2,1,0:T(8,128)} %s_any.1, f32[2,3,8,64,421]{4,3,2,1,0:T(8,128)} %k_any.1, ...), custom_call_target="tpu_custom_call" | custom-call | tf_op jit(solution)/shard_map/pallas_call | solution.py:379
  6.1 2.6 %copy-done = f32[2,3,8,64,421]{4,3,2,1,0:T(8,128)} copy-done((f32[2,3,8,64,421]{4,3,2,1,0:T(8,128)}, f32[2,3,8,64,421]{4,3,2,1,0:T(8,128)S(1)}, u32[]{:S(2)}) %copy-start) | copy-done | bytes 5173272
  8.8 11.1 %all-to-all-start = ((f32[32,8,128]{2,1,0:T(8,128)}), f32[32,8,128]{2,1,0:T(8,128)S(1)}, u32[]{:S(2)}, u32[]{:S(2)}) async-start(f32[32,8,128]{2,1,0:T(8,128)} %get-tuple-element.24), calls=%async_computation | async-start | bytes 262144 | tf_op jit(solution)/shard_map/all_to_all | solution.py:388
  19.9 0.3 collective-permute-start
  20.2 3.4 %collective-permute-start.1 = (f32[8,512]{1,0:T(8,128)S(1)}, f32[8,512]{1,0:T(8,128)S(1)}, u32[]{:S(2)}, u32[]{:S(2)}) collective-permute-start(f32[8,512]{1,0:T(8,128)S(1)} %get-tuple-element.26), channel_id=1, source_target_pairs={{8,16},{16,8},{24,32},{32,24},{40,48},{48,40},{56,64},{64,56},{72,... | collective-permute-start | bytes 49160 | tf_op jit(solution)/shard_map/ppermute | solution.py:387
  23.6 5.5 %all-to-all-done.parts_ref = f32[32,8,128]{2,1,0:T(8,128)S(1)} async-done(((f32[32,8,128]{2,1,0:T(8,128)}), f32[32,8,128]{2,1,0:T(8,128)S(1)}, u32[]{:S(2)}, u32[]{:S(2)}) %all-to-all-start) | async-done | bytes 131104 | tf_op jit(solution)/shard_map/all_to_all | solution.py:388
  29.2 14.4 %all_to_all.50.r_ref = f32[32,8,128]{2,1,0:T(8,128)S(1)} all-to-all(f32[32,8,128]{2,1,0:T(8,128)S(1)} %shard_map.69), channel_id=1, replica_groups=mesh['param'=32,'sensor'=8] {'param'}, dimensions={0} | all-to-all | bytes 262144 | tf_op jit(solution)/shard_map/all_to_all | solution.py:397
  43.6 2.8 %copy-done.1 = f32[2,3,8,64,421]{4,3,2,1,0:T(8,128)S(1)} copy-done((f32[2,3,8,64,421]{4,3,2,1,0:T(8,128)S(1)}, f32[2,3,8,64,421]{4,3,2,1,0:T(8,128)}, u32[]{:S(2)}) %copy-start.1) | copy-done | bytes 5173272
  46.4 2.6 %shard_map.70 = (f32[8,10,8,128]{3,2,1,0:T(8,128)S(1)}, f32[64,420]{1,0:T(8,128)}) custom-call(f32[32,8,128]{2,1,0:T(8,128)S(1)} %all_to_all.50.r_ref, f32[8,512]{1,0:T(8,128)S(1)} %collective-permute-done.inner_ref, f32[8,512]{1,0:T(8,128)S(1)} %collective-permute-done.1.outer_ref, f32[2,3,8,64,421]{4,3,2,1,0:T(8,128)S(1)} %copy-done.1, ...), custom_call_target="tpu_custom_call" | custom-call | tf_op jit(solution)/shard_map/pallas_call | solution.py:398
  49.0 15.5 %all_to_all.51.parts_ref = f32[8,10,8,128]{3,2,1,0:T(8,128)S(1)} all-to-all(f32[8,10,8,128]{3,2,1,0:T(8,128)S(1)} %get-tuple-element.33), channel_id=1, replica_groups=mesh['param'=32,'sensor'=8] {'sensor'}, dimensions={0} | all-to-all | bytes 655360 | tf_op jit(solution)/shard_map/all_to_all | solution.py:402
  64.6 1.9 %shard_map.71 = (f32[32,8,128]{2,1,0:T(8,128)S(1)}, f32[24,512]{1,0:T(8,128)S(1)}) custom-call(f32[8,10,8,128]{3,2,1,0:T(8,128)S(1)} %all_to_all.51.parts_ref, f32[24,512]{1,0:T(8,128)S(1)} %get-tuple-element.23.s_ref, f32[2,3,8,64,421]{4,3,2,1,0:T(8,128)S(1)} %copy-done.2, bf16[512,1024]{1,0:T(8,128)(2,1)S(1)} %get-tuple-element.31.high_ref, ...), custom_call_target="tpu_custom_call" | custom-call | tf_op jit(solution)/shard_map/pallas_call | solution.py:401
  66.5 13.2 %all_to_all.52.parts_ref = f32[32,8,128]{2,1,0:T(8,128)S(1)} all-to-all(f32[32,8,128]{2,1,0:T(8,128)S(1)} %get-tuple-element.35), channel_id=1, replica_groups=mesh['param'=32,'sensor'=8] {'param'}, dimensions={0} | all-to-all | bytes 262144 | tf_op jit(solution)/shard_map/all_to_all | solution.py:405
  79.7 0.3 shard_map.72
  80.0 18.0 %all_to_all.53 = f32[256,1,128]{2,1,0:T(1,128)S(1)} all-to-all(f32[256,1,128]{2,1,0:T(1,128)S(1)} %bitcast.10), channel_id=1, replica_groups=mesh['param'=32,'sensor'=8] {'param','sensor'}, dimensions={0} | all-to-all | bytes 262144 | tf_op jit(solution)/shard_map/all_to_all | solution.py:407
  98.1 2.2 %shard_map.73 = (f32[32,8,128]{2,1,0:T(8,128)S(1)}, f32[24,512]{1,0:T(8,128)S(1)}, f32[8,512]{1,0:T(8,128)S(1)}, f32[8,512]{1,0:T(8,128)S(1)}) custom-call(f32[24,512]{1,0:T(8,128)S(1)} %get-tuple-element.23.s_ref, f32[24,512]{1,0:T(8,128)S(1)} %get-tuple-element.34.g_ref, f32[32,8,128]{2,1,0:T(8,128)S(1)} %bitcast.8, ...), custom_call_target="tpu_custom_call" | custom-call | tf_op jit(solution)/shard_map/pallas_call | solution.py:390
  100.2 13.0 %all_to_all.54.parts_ref = f32[32,8,128]{2,1,0:T(8,128)S(1)} all-to-all(f32[32,8,128]{2,1,0:T(8,128)S(1)} %get-tuple-element.37), channel_id=1, replica_groups=mesh['param'=32,'sensor'=8] {'param'}, dimensions={0} | all-to-all | bytes 262144 | tf_op jit(solution)/shard_map/all_to_all | solution.py:393
  113.3 12.4 %all_to_all.55.r_ref = f32[32,8,128]{2,1,0:T(8,128)S(1)} all-to-all(f32[32,8,128]{2,1,0:T(8,128)S(1)} %shard_map.74), channel_id=1, replica_groups=mesh['param'=32,'sensor'=8] {'param'}, dimensions={0} | all-to-all | bytes 262144 | tf_op jit(solution)/shard_map/all_to_all | solution.py:397
  125.8 2.5 %shard_map.75 = (f32[8,10,8,128]{3,2,1,0:T(8,128)S(1)}, f32[64,420]{1,0:T(8,128)}) custom-call(f32[32,8,128]{2,1,0:T(8,128)S(1)} %all_to_all.55.r_ref, f32[8,512]{1,0:T(8,128)S(1)} %get-tuple-element.38.inner_ref, f32[8,512]{1,0:T(8,128)S(1)} %get-tuple-element.39.outer_ref, f32[2,3,8,64,421]{4,3,2,1,0:T(8,128)S(1)} %copy-done.2, ...), custom_call_target="tpu_custom_call" | custom-call | tf_op jit(solution)/shard_map/pallas_call | solution.py:398
  128.3 12.4 %all_to_all.56.parts_ref = f32[8,10,8,128]{3,2,1,0:T(8,128)S(1)} all-to-all(f32[8,10,8,128]{3,2,1,0:T(8,128)S(1)} %get-tuple-element.40), channel_id=1, replica_groups=mesh['param'=32,'sensor'=8] {'sensor'}, dimensions={0} | all-to-all | bytes 655360 | tf_op jit(solution)/shard_map/all_to_all | solution.py:402
  140.7 1.9 %shard_map.76 = (f32[32,8,128]{2,1,0:T(8,128)S(1)}, f32[24,512]{1,0:T(8,128)S(1)}) custom-call(f32[8,10,8,128]{3,2,1,0:T(8,128)S(1)} %all_to_all.56.parts_ref, f32[24,512]{1,0:T(8,128)S(1)} %get-tuple-element.36.s_ref, f32[2,3,8,64,421]{4,3,2,1,0:T(8,128)S(1)} %copy-done.2, bf16[512,1024]{1,0:T(8,128)(2,1)S(1)} %get-tuple-element.31.high_ref, ...), custom_call_target="tpu_custom_call" | custom-call | tf_op jit(solution)/shard_map/pallas_call | solution.py:401
  142.6 13.2 %all_to_all.57.parts_ref = f32[32,8,128]{2,1,0:T(8,128)S(1)} all-to-all(f32[32,8,128]{2,1,0:T(8,128)S(1)} %get-tuple-element.42), channel_id=1, replica_groups=mesh['param'=32,'sensor'=8] {'param'}, dimensions={0} | all-to-all | bytes 262144 | tf_op jit(solution)/shard_map/all_to_all | solution.py:405
  155.8 0.3 shard_map.77
  156.1 18.0 %all_to_all.58 = f32[256,1,128]{2,1,0:T(1,128)S(1)} all-to-all(f32[256,1,128]{2,1,0:T(1,128)S(1)} %bitcast.11), channel_id=1, replica_groups=mesh['param'=32,'sensor'=8] {'param','sensor'}, dimensions={0} | all-to-all | bytes 262144 | tf_op jit(solution)/shard_map/all_to_all | solution.py:407
  174.2 0.9 shard_map.78
  (10 shorter events, 0.1 us)
Async XLA Ops:
  0.6 28.5 %copy-start.3 = (f32[64,420]{1,0:T(8,128)S(1)}, f32[64,420]{1,0:T(8,128)}, u32[]{:S(2)}) copy-start(f32[64,420]{1,0:T(8,128)} %observed_ref.3) | copy-start | bytes 322564
  6.1 2.6 %copy-start = (f32[2,3,8,64,421]{4,3,2,1,0:T(8,128)}, f32[2,3,8,64,421]{4,3,2,1,0:T(8,128)S(1)}, u32[]{:S(2)}) copy-start(f32[2,3,8,64,421]{4,3,2,1,0:T(8,128)S(1)} %get-tuple-element.30.k_ref) | copy-start | bytes 15519748
  8.8 20.4 %all-to-all-start = ((f32[32,8,128]{2,1,0:T(8,128)}), f32[32,8,128]{2,1,0:T(8,128)S(1)}, u32[]{:S(2)}, u32[]{:S(2)}) async-start(f32[32,8,128]{2,1,0:T(8,128)} %get-tuple-element.24), calls=%async_computation | async-start | bytes 262144 | tf_op jit(solution)/shard_map/all_to_all | solution.py:388
  19.9 9.3 %collective-permute-start = (f32[8,512]{1,0:T(8,128)S(1)}, f32[8,512]{1,0:T(8,128)S(1)}, u32[]{:S(2)}, u32[]{:S(2)}) collective-permute-start(f32[8,512]{1,0:T(8,128)S(1)} %get-tuple-element.25), channel_id=1, source_target_pairs={{0,8},{8,0},{16,24},{24,16},{32,40},{40,32},{48,56},{56,48},{64,72... | collective-permute-start | bytes 49160 | tf_op jit(solution)/shard_map/ppermute | solution.py:386
  20.2 9.0 %collective-permute-start.1 = (f32[8,512]{1,0:T(8,128)S(1)}, f32[8,512]{1,0:T(8,128)S(1)}, u32[]{:S(2)}, u32[]{:S(2)}) collective-permute-start(f32[8,512]{1,0:T(8,128)S(1)} %get-tuple-element.26), channel_id=1, source_target_pairs={{8,16},{16,8},{24,32},{32,24},{40,48},{48,40},{56,64},{64,56},{72,... | collective-permute-start | bytes 49160 | tf_op jit(solution)/shard_map/ppermute | solution.py:387
  43.6 2.8 %copy-start.1 = (f32[2,3,8,64,421]{4,3,2,1,0:T(8,128)S(1)}, f32[2,3,8,64,421]{4,3,2,1,0:T(8,128)}, u32[]{:S(2)}) copy-start(f32[2,3,8,64,421]{4,3,2,1,0:T(8,128)} %copy-done) | copy-start | bytes 15519748
  46.4 18.1 %copy-start.2 = (f32[2,3,8,64,421]{4,3,2,1,0:T(8,128)S(1)}, f32[2,3,8,64,421]{4,3,2,1,0:T(8,128)}, u32[]{:S(2)}) copy-start(f32[2,3,8,64,421]{4,3,2,1,0:T(8,128)} %copy-done) | copy-start | bytes 15519748
